TPU v7x, 32 devices: a whole 2x2x4 slice. The times are simulated.
32 devices in a mesh: groups: 2 (over x), seq: 8 (over z, y), exp: 2 (over core).
Axes of the slice: x: 2, y: 2, z: 4, core: 2. Of those that a mesh axis runs over, the one named last changes fastest.
Arguments:
- stream: bfloat16 [2048, 2048], P(('groups', 'seq', 'exp')), parts along dimension 0, may hold values from -5 to 5
- queries: bfloat16 [2048, 4096], P(('groups', 'seq'), 'exp'), parts along dimension 0, may hold values from -131 to 131
- key_rows: bfloat16 [2048, 512], P(('groups', 'seq'), 'exp'), parts along dimension 0, may hold values from -4 to 4
- value_rows: bfloat16 [2048, 512], P(('groups', 'seq'), 'exp'), parts along dimension 0, may hold values from -4 to 4
- out_weight: bfloat16 [2048, 4096], P('seq', 'exp'), may hold values from -0.375 to 0.375
- norm_gain: float32 [2048], replicated, may hold values from 0.1 to 1.9
- expert_ids: int32 [2048, 8], P(('groups', 'seq', 'exp')), parts along dimension 0, may hold values from 0 to 63, all different within a row; in each aligned block of 64 rows (0 to 63, 64 to 127, ...) at most 12 rows name the same one
- gate_weights: float32 [2048, 8], P(('groups', 'seq', 'exp')), parts along dimension 0, may hold values from 0.05 to 0.5
- expert_in: bfloat16 [64, 2048, 1536], P(('seq', 'exp')), may hold values from -0.125 to 0.125
- expert_out: bfloat16 [64, 768, 2048], P(('seq', 'exp')), may hold values from -0.21875 to 0.21875
Outputs:
- layer_out: bfloat16 [2048, 2048], P(('groups', 'seq', 'exp')), parts along dimension 0
There are 2 independent parts, one for each index of `groups`. A program takes and returns all parts, laid end to end along the dimension named above; an argument that names none is the same for every part. Nothing has to cross between parts.
Inputs may be any that keep to these rules, and one draw needn't show every extreme that they name: `expert_ids`: each row names 8 different experts. Among the 64 rows of one device (aligned blocks of rows), no expert is named more than 12 times, a bound that some block reaches.
All inputs are finite; a program needn't handle non-finite values.
Results may differ from a plain program's by a relative error of at most 0.0095.
Values may be sent and summed in bfloat16 or wider, within the bound.
A program may use at most 128 MiB of HBM per device.

v0:
```python
import jax
import jax.numpy as jnp
from jax import lax
from jax.sharding import PartitionSpec as P

HD = 128
EXPERTS = 64
TOPK = 8
CAP = 12


neg_large = -1e30


def attend_piece(state, query_group, key_piece, value_piece, key_start, query_start):
    largest, total, summed = state
    length = key_piece.shape[0]
    groups = query_group.shape[1]
    head_size = query_group.shape[3]
    rows = query_group.shape[0]
    keyed = key_piece.reshape(length, groups, head_size)
    valued = value_piece.reshape(length, groups, head_size)
    scores = jnp.einsum(
        "tghd,sgd->gths", query_group, keyed, preferred_element_type=jnp.float32
    ) / jnp.sqrt(jnp.float32(head_size))
    query_pos = query_start + jnp.arange(rows, dtype=jnp.int32)
    key_pos = key_start + jnp.arange(length, dtype=jnp.int32)
    allowed = (key_pos[None, :] <= query_pos[:, None])[None, :, None, :]
    scores = jnp.where(allowed, scores, neg_large)
    new_largest = jnp.maximum(largest, jnp.max(scores, axis=-1))
    rescale = jnp.exp(largest - new_largest)
    exps = jnp.where(allowed, jnp.exp(scores - new_largest[..., None]), 0.0)
    total = total * rescale + jnp.sum(exps, axis=-1)
    summed = summed * rescale[..., None] + jnp.einsum(
        "gths,sgd->gthd", exps.astype(jnp.bfloat16), valued, preferred_element_type=jnp.float32
    )
    return (new_largest, total, summed)


def on_device(
    stream,
    queries,
    key_rows,
    value_rows,
    out_weight,
    norm_gain,
    expert_ids,
    gate_weights,
    expert_in,
    expert_out,
):
    rows = queries.shape[0]
    local_groups = key_rows.shape[1] // HD
    per_group = queries.shape[1] // (local_groups * HD)
    query_group = queries.reshape(rows, local_groups, per_group, HD)
    query_start = lax.axis_index("seq") * rows
    initial = (
        jnp.full((local_groups, rows, per_group), neg_large, jnp.float32),
        jnp.zeros((local_groups, rows, per_group), jnp.float32),
        jnp.zeros((local_groups, rows, per_group, HD), jnp.float32),
    )
    state = initial
    key_piece = lax.all_gather(key_rows, "seq", axis=0, tiled=True)
    value_piece = lax.all_gather(value_rows, "seq", axis=0, tiled=True)
    length = key_piece.shape[0]
    count = length // 512
    key_blocks = key_piece.reshape(count, 512, key_piece.shape[1])
    value_blocks = value_piece.reshape(count, 512, value_piece.shape[1])
    offsets = jnp.arange(count, dtype=jnp.int32) * 512

    def step(carry, block):
        return (attend_piece(carry, query_group, block[0], block[1], block[2], query_start), None)

    state, unused = lax.scan(step, state, (key_blocks, value_blocks, offsets))
    largest, total, summed = state
    context = (
        (summed / total[..., None]).transpose(1, 0, 2, 3).reshape(rows, -1).astype(jnp.bfloat16)
    )
    seq_count = lax.axis_size("seq")
    exp_count = lax.axis_size("exp")
    local_rows = stream.shape[0]
    partial_heads = lax.dot_general(
        context,
        lax.all_gather(out_weight, "seq", axis=0, tiled=True),
        (((1,), (1,)), ((), ())),
        preferred_element_type=jnp.float32,
    )
    attn_out = lax.psum_scatter(
        partial_heads.astype(jnp.bfloat16), "exp", scatter_dimension=0, tiled=True
    ).astype(jnp.float32)
    mixed = stream.astype(jnp.float32) + attn_out
    normed = (
        mixed * lax.rsqrt(jnp.mean(mixed * mixed, axis=-1, keepdims=True) + 1e-06) * norm_gain
    ).astype(jnp.bfloat16)
    width = normed.shape[1]
    flat_ids = expert_ids.reshape(-1)
    onehot = (flat_ids[:, None] == jnp.arange(EXPERTS, dtype=jnp.int32)[None, :]).astype(jnp.int32)
    earlier = jnp.cumsum(onehot, axis=0) - onehot
    slots = jnp.sum(earlier * onehot, axis=1)
    destination = flat_ids * CAP + slots
    chooser = (destination[None, :] == jnp.arange(EXPERTS * CAP, dtype=jnp.int32)[:, None]).astype(
        jnp.int32
    )
    chooser = jnp.sum(chooser.reshape(EXPERTS * CAP, local_rows, TOPK), axis=-1).astype(
        jnp.bfloat16
    )
    outgoing = (
        jnp.dot(chooser, normed, preferred_element_type=jnp.float32)
        .astype(jnp.bfloat16)
        .reshape(EXPERTS, CAP, width)
    )
    local_experts = expert_in.shape[0]
    hidden_units = expert_out.shape[1]
    sectioned = outgoing.reshape(seq_count, exp_count, local_experts, CAP, width)
    arrived = lax.all_to_all(
        lax.all_to_all(sectioned, "seq", split_axis=0, concat_axis=0, tiled=True),
        "exp",
        split_axis=1,
        concat_axis=1,
        tiled=True,
    )
    received = arrived.reshape(-1, CAP, width)
    senders = received.shape[0] // local_experts
    slots_here = received.shape[1]
    arranged = received.reshape(senders, local_experts, slots_here, width)
    gate_up = jnp.einsum("secd,edf->secf", arranged, expert_in, preferred_element_type=jnp.float32)
    act = (jax.nn.silu(gate_up[..., :hidden_units]) * gate_up[..., hidden_units:]).astype(
        jnp.bfloat16
    )
    result = jnp.einsum(
        "secf,efd->secd", act, expert_out, preferred_element_type=jnp.float32
    ).astype(jnp.bfloat16)
    finished = result.reshape(received.shape).reshape(sectioned.shape)
    back = lax.all_to_all(
        lax.all_to_all(finished, "seq", split_axis=0, concat_axis=0, tiled=True),
        "exp",
        split_axis=1,
        concat_axis=1,
        tiled=True,
    ).reshape(EXPERTS, CAP, width)
    picked = back.reshape(EXPERTS * CAP, width)[destination].reshape(local_rows, TOPK, width)
    combined = jnp.sum(gate_weights[..., None] * picked.astype(jnp.float32), axis=1)
    return (mixed + combined).astype(jnp.bfloat16)


def solution(mesh):
    in_specs = (
        P(("groups", "seq", "exp"), None),
        P(("groups", "seq"), "exp"),
        P(("groups", "seq"), "exp"),
        P(("groups", "seq"), "exp"),
        P("seq", "exp"),
        P(),
        P(("groups", "seq", "exp"), None),
        P(("groups", "seq", "exp"), None),
        P(("seq", "exp"), None, None),
        P(("seq", "exp"), None, None),
    )
    out_specs = P(("groups", "seq", "exp"), None)
    return jax.shard_map(
        on_device, mesh=mesh, in_specs=in_specs, out_specs=out_specs, check_vma=False
    )
```

profile of v0, /device:TPU:16, one launch (start us, length us, event | category | flops | bytes accessed | tf_op | source)
XLA Modules:
  0.0 387.3 jit_solution(11619472551129220449)
XLA Ops:
  6.5 0.0 all-gather.2.cloned.1.call-start
  6.5 0.7 all-gather.2.cloned.1.call-update
  7.3 0.0 reduce-scatter.2.cloned.1.call-start
  7.3 1.3 copy.66
  8.7 0.3 copy.68
  9.0 29.8 %all_gather.9 = bf16[1024,256]{1,0:T(8,128)(2,1)S(1)} all-gather(bf16[128,256]{1,0:T(8,128)(2,1)} %param.14), channel_id=1, replica_groups=mesh['groups'=2,'seq'=8,'exp'=2] {'seq'}, dimensions={0}, use_global_device_ids=true | all-gather | bytes 589824 | tf_op jit(solution)/shard_map/all_gather | solution.py:63
  38.8 34.0 %all_gather.10 = bf16[1024,256]{1,0:T(8,128)(2,1)S(1)} all-gather(bf16[128,256]{1,0:T(8,128)(2,1)} %param.15), channel_id=1, replica_groups=mesh['groups'=2,'seq'=8,'exp'=2] {'seq'}, dimensions={0}, use_global_device_ids=true | all-gather | bytes 589824 | tf_op jit(solution)/shard_map/all_gather | solution.py:64
  72.8 23.1 %while.15 = (s32[]{:T(128)}, f32[2,128,8]{1,2,0:T(8,128)S(1)}, f32[2,128,8]{1,2,0:T(8,128)S(1)}, f32[2,128,8,128]{3,1,2,0:T(8,128)S(1)}, s32[2]{0:T(128)S(1)}, /...) while((s32[]{:T(128)}, f32[2,128,8]{1,2,0:T(8,128)S(1)}, ...), condition=%wide.region_3.4_spmd.clone, body=%wide.region_0.3_spmd.clone.sunk | while | flops 551365248 | bytes 18224280 | solution.py:74
  72.8 0.6 dynamic_slice.19
  73.4 0.6 iota_add_fusion.5
  74.0 0.1 broadcast_compare_fusion.2
  74.1 0.1 copy.98
  74.3 2.8 fusion.57
  77.1 3.2 fusion.58
  80.4 0.1 copy.99
  80.5 3.9 fusion.60
  84.4 0.6 dynamic_slice.19
  85.0 0.6 iota_add_fusion.5
  85.5 0.1 broadcast_compare_fusion.2
  85.7 0.1 copy.98
  85.9 2.8 fusion.57
  88.7 3.2 fusion.58
  91.9 0.1 copy.99
  92.0 3.9 fusion.60
  95.9 0.3 copy.70
  96.3 0.1 divide_convert_fusion
  96.4 45.5 %all-gather.2.cloned.1.call-done = bf16[2048,2048]{1,0:T(8,128)(2,1)} async-done(((bf16[256,2048]{1,0:T(8,128)(2,1)}), bf16[2048,2048]{1,0:T(8,128)(2,1)}) %all-gather.2.cloned.1.call-update) | async-done | bytes 8388624 | tf_op jit(solution)/shard_map/all_gather | solution.py:84
  141.9 7.2 %convolution_convert_fusion.1 = bf16[128,2048]{1,0:T(8,128)(2,1)} fusion(bf16[128,2048]{0,1:T(8,128)(2,1)S(1)} %bitcast.106, bf16[2048,2048]{1,0:T(8,128)(2,1)} %all-gather.2.cloned.1.call-done), kind=kOutput, calls=%fused_computation.32 | convolution fusion | flops 1074003968 | bytes 9437184 | tf_op jit(solution)/shard_map/dot_general | solution.py:82
  149.1 0.0 reduce-scatter.2.cloned.1.call-update
  149.1 0.0 copy-done.2
  149.1 0.1 copy.72
  149.2 0.1 eq.39
  149.3 0.1 eq.43
  149.4 1.2 reduce-window.6
  150.6 0.2 slice_reduce_fusion
  150.9 0.1 fusion.34
  151.0 0.1 reduce_sum.50
  151.1 1.2 convert_reduce_fusion
  152.3 4.2 %reduce-scatter.2.cloned.1.call-done = bf16[64,2048]{1,0:T(8,128)(2,1)} async-done(((bf16[128,2048]{1,0:T(8,128)(2,1)}), bf16[64,2048]{1,0:T(8,128)(2,1)}) %reduce-scatter.2.cloned.1.call-update) | async-done | bytes 262160 | tf_op jit(solution)/shard_map/reduce_scatter | solution.py:88
  156.6 0.0 copy-done
  156.6 1.1 multiply_reduce_fusion
  157.7 0.0 copy-done.1
  157.7 2.1 convolution_convert_fusion
  159.8 2.7 reshape_reshape.12
  162.5 4.9 %copy.76 = bf16[8,2,4,12,2048]{4,2,3,1,0:T(4,128)(2,1)S(1)} copy(bf16[8,2,4,12,2048]{4,3,2,1,0:T(8,128)(2,1)} %reshape_reshape.12) | data formatting | bytes 6291456 | tf_op jit(solution)/shard_map/reshape;reshape | solution.py:114
  167.4 75.0 %all_to_all.20 = bf16[8,2,4,12,2048]{4,2,3,1,0:T(4,128)(2,1)S(1)} all-to-all(bf16[8,2,4,12,2048]{4,2,3,1,0:T(4,128)(2,1)S(1)} %copy.76), channel_id=1, replica_groups=mesh['groups'=2,'seq'=8,'exp'=2] {'seq'}, dimensions={0} | all-to-all | bytes 6291456 | tf_op jit(solution)/shard_map/all_to_all | solution.py:116
  242.4 1.7 copy.77
  244.2 6.3 %all_to_all.21 = bf16[8,2,4,12,2048]{4,0,3,2,1:T(8,128)(2,1)S(1)} all-to-all(bf16[8,2,4,12,2048]{4,0,3,2,1:T(8,128)(2,1)S(1)} %copy.77), channel_id=1, replica_groups=mesh['groups'=2,'seq'=8,'exp'=2] {'exp'}, dimensions={1} | all-to-all | bytes 6291456 | tf_op jit(solution)/shard_map/all_to_all | solution.py:115
  250.4 4.9 %copy.78 = bf16[8,2,4,12,2048]{4,1,0,3,2:T(2,128)(2,1)} copy(bf16[8,2,4,12,2048]{4,0,3,2,1:T(8,128)(2,1)S(1)} %all_to_all.21) | data formatting | bytes 6291456 | tf_op jit(solution)/shard_map/all_to_all | solution.py:115
  255.4 4.0 %reshape_reshape.13 = bf16[16,4,12,2048]{3,0,2,1:T(8,128)(2,1)S(1)} reshape(bf16[8,2,4,12,2048]{4,1,0,3,2:T(2,128)(2,1)} %copy.78) | data formatting | bytes 6291456 | tf_op jit(solution)/shard_map/reshape;reshape | solution.py:125
  259.4 10.8 %fusion.18 = f32[16,4,12,1536]{3,0,2,1:T(8,128)S(1)} fusion(bf16[16,4,12,2048]{3,0,2,1:T(8,128)(2,1)S(1)} %reshape_reshape.13, bf16[4,2048,1536]{2,1,0:T(8,128)(2,1)} %param.20), kind=kOutput, calls=%fused_computation.28 | convolution fusion | flops 4831838208 | bytes 33030144 | tf_op jit(solution)/shard_map/secd,edf->secf/dot_general | solution.py:126
  270.2 7.5 %fusion.24 = bf16[16,4,12,2048]{3,0,2,1:T(8,128)(2,1)S(1)} fusion(bf16[4,768,2048]{2,1,0:T(8,128)(2,1)} %param.21, f32[16,4,12,1536]{3,0,2,1:T(8,128)S(1)} %fusion.18), kind=kOutput, calls=%fused_computation.31 | convolution fusion | flops 2421030912 | bytes 20447232 | tf_op jit(solution)/shard_map/secf,efd->secd/dot_general | solution.py:130
  277.7 4.1 %copy.87 = bf16[16,4,12,2048]{3,1,2,0:T(4,128)(2,1)} copy(bf16[16,4,12,2048]{3,0,2,1:T(8,128)(2,1)S(1)} %fusion.24) | data formatting | bytes 6291456 | tf_op jit(solution)/shard_map/reshape;reshape | solution.py:133
  281.8 5.7 %all-to-all-start.2 = ((bf16[8,2,4,12,2048]{4,2,3,1,0:T(4,128)(2,1)}), bf16[8,2,4,12,2048]{4,2,3,1,0:T(4,128)(2,1)S(1)}, u32[]{:S(2)}, u32[]{:S(2)}) async-start(bf16[8,2,4,12,2048]{4,2,3,1,0:T(4,128)(2,1)} %bitcast.102), calls=%async_computation.3 | async-start | bytes 6291456 | tf_op jit(solution)/shard_map/all_to_all | solution.py:135
  287.5 0.1 mul.87
  287.6 0.1 copy.71
  287.7 67.8 %all-to-all-done.2 = bf16[8,2,4,12,2048]{4,2,3,1,0:T(4,128)(2,1)S(1)} async-done(((bf16[8,2,4,12,2048]{4,2,3,1,0:T(4,128)(2,1)}), bf16[8,2,4,12,2048]{4,2,3,1,0:T(4,128)(2,1)S(1)}, u32[]{:S(2)}, u32[]{:S(2)}) %all-to-all-start.2) | async-done | bytes 3145760 | tf_op jit(solution)/shard_map/all_to_all | solution.py:135
  355.5 1.7 copy.80
  357.2 6.3 %all_to_all.22 = bf16[8,2,4,12,2048]{4,0,3,2,1:T(8,128)(2,1)S(1)} all-to-all(bf16[8,2,4,12,2048]{4,0,3,2,1:T(8,128)(2,1)S(1)} %copy.80), channel_id=1, replica_groups=mesh['groups'=2,'seq'=8,'exp'=2] {'exp'}, dimensions={1} | all-to-all | bytes 6291456 | tf_op jit(solution)/shard_map/all_to_all | solution.py:134
  363.5 3.7 copy.81
  367.2 4.7 %reshape_reshape.15 = bf16[768,2048]{1,0:T(8,128)(2,1)S(1)} reshape(bf16[8,2,4,12,2048]{4,3,2,1,0:T(8,128)(2,1)} %copy.81) | data formatting | bytes 6291456 | tf_op jit(solution)/shard_map/reshape;reshape | solution.py:141
  371.9 3.3 gather_fusion
  375.2 3.4 fusion.17
  378.7 1.8 add_convert_fusion
  (26 shorter events, 0.2 us)
Async XLA Ops:
  6.5 135.3 %all-gather.2.cloned.1.call-start = ((), (), s32[]{:S(2)}) async-start(), calls=%async_computation.5 | async-start | bytes 9437184 | tf_op jit(solution)/shard_map/all_gather | solution.py:84
  7.3 149.3 %reduce-scatter.2.cloned.1.call-start = ((), (), s32[]{:S(2)}) async-start(), calls=%async_computation.6 | async-start | bytes 786432 | tf_op jit(solution)/shard_map/reduce_scatter | solution.py:88
  141.9 7.2 %copy-start.2 = (s32[64,8]{0,1:T(8,128)S(1)}, s32[64,8]{0,1:T(8,128)}, u32[]{:S(2)}) copy-start(s32[64,8]{0,1:T(8,128)} %param.18) | copy-start | bytes 6148
  141.9 14.7 %copy-start = (bf16[64,2048]{1,0:T(8,128)(2,1)S(1)}, bf16[64,2048]{1,0:T(8,128)(2,1)}, u32[]{:S(2)}) copy-start(bf16[64,2048]{1,0:T(8,128)(2,1)} %param.12) | copy-start | bytes 786436
  141.9 15.8 %copy-start.1 = (f32[2048]{0:T(1024)S(1)}, f32[2048]{0:T(1024)}, u32[]{:S(2)}) copy-start(f32[2048]{0:T(1024)} %param.17) | copy-start | bytes 24580
  281.8 5.8 %copy-start.3 = (f32[64,8]{0,1:T(8,128)S(1)}, f32[64,8]{0,1:T(8,128)}, u32[]{:S(2)}) copy-start(f32[64,8]{0,1:T(8,128)} %param.19) | copy-start | bytes 6148
  281.8 73.7 %all-to-all-start.2 = ((bf16[8,2,4,12,2048]{4,2,3,1,0:T(4,128)(2,1)}), bf16[8,2,4,12,2048]{4,2,3,1,0:T(4,128)(2,1)S(1)}, u32[]{:S(2)}, u32[]{:S(2)}) async-start(bf16[8,2,4,12,2048]{4,2,3,1,0:T(4,128)(2,1)} %bitcast.102), calls=%async_computation.3 | async-start | bytes 6291456 | tf_op jit(solution)/shard_map/all_to_all | solution.py:135
Sparse Core Ops, SparseCore 0:
  9.5 132.3 all-gather.1
  149.2 7.2 reduce-scatter.1
where the time goes:
time: 393 us; the launch traced here: 387 us
  blocking collectives  151 us (38%)
  waiting for transfers between devices  118 us (30%)
  matrix products  40.9 us (10%)
  local copies, waits for them, and re-layouts  40.3 us (10%)
  other arithmetic  16.9 us (4%)
  between operations  13.6 us (3%)
  starting transfers between devices  5.77 us (1%)
    all_to_all x1, blocking collectives, on_device(): lax.all_to_all(sectioned, 'seq', split_axis=0, concat_axis=0, tiled=True)  75 us
    all_to_all x1, waiting for transfers between devices, on_device(): lax.all_to_all(finished, 'seq', split_axis=0, concat_axis=0, tiled=True)  67.8 us
    all_gather x1, waiting for transfers between devices, on_device(): lax.all_gather(out_weight, 'seq', axis=0, tiled=True)  45.5 us
    all_gather x1, blocking collectives, on_device(): value_piece = lax.all_gather(value_rows, 'seq', axis=0, tiled=True)  34 us
    all_gather x1, blocking collectives, on_device(): key_piece = lax.all_gather(key_rows, 'seq', axis=0, tiled=True)  29.8 us
    dot_general x1, matrix products, on_device(): jnp.einsum('secd,edf->secf', arranged, expert_in, preferred_element_type=...  10.8 us
  transfers between devices with their start and end apart: 3, of which 3 were waited for; matrix products, arithmetic and copies ran while one was open for 7% of the time, Pallas kernels for 0%

commit v1 on v0

v1 whole, which is shorter than its diff:
```python
import functools

import jax
import jax.numpy as jnp
from jax import lax
from jax.experimental import pallas as pl
from jax.experimental.pallas import tpu as pltpu
from jax.sharding import PartitionSpec as P

HD = 128
EXPERTS = 64
CAP = 12
LOW = 2
PARTS = 2
VMEM_LIMIT = 60 * 1024 * 1024
neg_large = -1e30


def split_position():
    seq = lax.axis_index("seq")
    return seq // LOW, seq % LOW, lax.axis_index("exp")


def line_barrier(high, h, l, e):
    barrier = pltpu.get_barrier_semaphore()

    def greet(target):
        pl.semaphore_signal(barrier, inc=1, device_id=target, device_id_type=pl.DeviceIdType.MESH)

    @pl.when(h + 1 < high)
    def _():
        greet({"seq": (h + 1) * LOW + l})

    @pl.when(h > 0)
    def _():
        greet({"seq": (h - 1) * LOW + l})

    greet({"seq": h * LOW + 1 - l})
    greet({"exp": 1 - e})

    ends = jnp.where(h + 1 < high, 1, 0) + jnp.where(h > 0, 1, 0)
    pl.semaphore_wait(barrier, ends + 2)


def gather_steps(high, outs, cross, parts, recv, send, h, l, e):
    count = len(outs)

    def slot(a, h0, l0, e0, c):
        rows = outs[a].shape[-2] // parts[a]
        at = (h0, l0, e0) if cross[a] else (h0, l0)
        return outs[a].at[at + (pl.ds(c * rows, rows),)]

    def copy(a, h0, l0, e0, c, way):
        target = (
            {"seq": (h + 1) * LOW + l},
            {"seq": (h - 1) * LOW + l},
            {"seq": h * LOW + 1 - l},
            {"exp": 1 - e},
        )[way]
        ref = slot(a, h0, l0, e0, c)
        return pltpu.make_async_remote_copy(
            src_ref=ref,
            dst_ref=ref,
            send_sem=send[a].at[way, h0, l0, c],
            recv_sem=recv[a].at[h0, l0, e0, c],
            device_id=target,
            device_id_type=pl.DeviceIdType.MESH,
        )

    def pass_on(a, h0, c, right, left):
        if right:
            @pl.when(h + 1 < high)
            def _():
                copy(a, h0, l, e, c, 0).start()
        if left:
            @pl.when(h > 0)
            def _():
                copy(a, h0, l, e, c, 1).start()
        copy(a, h0, l, e, c, 2).start()
        if cross[a]:
            copy(a, h0, l, e, c, 3).start()

    def from_across(a, h0, c):
        copy(a, h0, 1 - l, e, c, 2).wait_recv()
        if cross[a]:
            copy(a, h0, 1 - l, e, c, 3).start()

    for a in range(count):
        for c in range(parts[a]):
            pass_on(a, h, c, True, True)
    for t in range(1, high + 1):
        if t < high:
            for a in range(count):
                for c in range(parts[a]):
                    @pl.when(h - t >= 0)
                    def _():
                        copy(a, h - t, l, e, c, 0).wait_recv()
                        pass_on(a, h - t, c, True, False)

                    @pl.when(h + t < high)
                    def _():
                        copy(a, h + t, l, e, c, 1).wait_recv()
                        pass_on(a, h + t, c, False, True)
        for a in range(count):
            for c in range(parts[a]):
                if t == 1:
                    from_across(a, h, c)
                else:
                    @pl.when(h - t + 1 >= 0)
                    def _():
                        from_across(a, h - t + 1, c)

                    @pl.when(h + t - 1 < high)
                    def _():
                        from_across(a, h + t - 1, c)
    for a in range(count):
        for c in range(parts[a]):
            for h0 in range(high):
                if cross[a]:
                    for l0 in range(LOW):
                        copy(a, h0, l0, 1 - e, c, 3).wait_recv()
                        copy(a, h0, l0, e, c, 3).wait_send()
                copy(a, h0, l, e, c, 2).wait_send()

                @pl.when((h + 1 < high) & (h0 <= h))
                def _():
                    copy(a, h0, l, e, c, 0).wait_send()

                @pl.when((h > 0) & (h0 >= h))
                def _():
                    copy(a, h0, l, e, c, 1).wait_send()


def gather_kernel(high, cross, parts, *refs):
    count = len(cross)
    ins, outs = refs[:count], refs[count : 2 * count]
    recv = refs[2 * count : 3 * count]
    send = refs[3 * count : 4 * count]
    local = refs[4 * count]
    h, l, e = split_position()
    copies = []
    for a in range(count):
        at = (h, l, e) if cross[a] else (h, l)
        copies.append(pltpu.make_async_copy(ins[a], outs[a].at[at], local.at[a]))
        copies[-1].start()
    line_barrier(high, h, l, e)
    for one in copies:
        one.wait()
    gather_steps(high, outs, cross, parts, recv, send, h, l, e)


def gather(arrays, cross, parts, high, collective_id):
    count = len(arrays)
    exp_count = 2
    outs = []
    for array, both in zip(arrays, cross):
        lead = (high, LOW, exp_count) if both else (high, LOW)
        outs.append(jax.ShapeDtypeStruct(lead + array.shape, array.dtype))
    whole = pl.BlockSpec(memory_space=pltpu.VMEM)
    return pl.pallas_call(
        functools.partial(gather_kernel, high, cross, parts),
        out_shape=tuple(outs),
        in_specs=[whole] * count,
        out_specs=tuple([whole] * count),
        scratch_shapes=[pltpu.SemaphoreType.DMA((high, LOW, exp_count, p)) for p in parts]
        + [pltpu.SemaphoreType.DMA((4, high, LOW, p)) for p in parts]
        + [pltpu.SemaphoreType.DMA((count,))],
        compiler_params=pltpu.CompilerParams(
            collective_id=collective_id, has_side_effects=True, vmem_limit_bytes=VMEM_LIMIT
        ),
        name="gather" + str(collective_id),
    )(*arrays)


def exchange_kernel(
    seq_count, part_ref, stream_ref, gain_ref, mixed_ref, normed_ref, mine, ready, landed, sem_a, sem_b, sem_c, sem_d
):
    me = lax.axis_index("seq")
    e = lax.axis_index("exp")
    features = part_ref.shape[-1]
    barrier = pltpu.get_barrier_semaphore()
    mesh_id = pl.DeviceIdType.MESH
    pl.semaphore_signal(barrier, inc=1, device_id={"exp": 1 - e}, device_id_type=mesh_id)
    for d in range(1, seq_count):
        pl.semaphore_signal(
            barrier, inc=1, device_id={"seq": (me + d) % seq_count}, device_id_type=mesh_id
        )
    pl.semaphore_wait(barrier, seq_count)

    def over(s):
        return pltpu.make_async_remote_copy(
            src_ref=part_ref.at[s, 1 - e],
            dst_ref=mine.at[s],
            send_sem=sem_a.at[s],
            recv_sem=sem_b.at[s],
            device_id={"exp": 1 - e},
            device_id_type=mesh_id,
        )

    def away(d, source):
        return pltpu.make_async_remote_copy(
            src_ref=ready.at[(me + d) % seq_count],
            dst_ref=landed.at[source],
            send_sem=sem_c.at[d],
            recv_sem=sem_d.at[source],
            device_id={"seq": (me + d) % seq_count},
            device_id_type=mesh_id,
        )

    order = list(range(1, seq_count)) + [0]
    for d in order:
        over((me + d) % seq_count).start()
    for d in order:
        s = (me + d) % seq_count
        over(s).wait_recv()
        total = part_ref[s, e].astype(jnp.float32) + mine[s].astype(jnp.float32)
        ready[s] = total.astype(ready.dtype)
        if d:
            away(d, me).start()
    landed[me] = ready[me]
    for d in range(1, seq_count):
        away(d, (me + seq_count - d) % seq_count).wait_recv()
    squares = None
    for s in range(seq_count):
        columns = pl.ds(s * features, features)
        value = stream_ref[:, columns].astype(jnp.float32) + landed[s].astype(jnp.float32)
        mixed_ref[:, columns] = value
        term = jnp.sum(value * value, axis=-1, keepdims=True)
        squares = term if squares is None else squares + term
    width = seq_count * features
    factor = lax.rsqrt(squares / width + 1e-06)
    for s in range(seq_count):
        columns = pl.ds(s * features, features)
        normed_ref[:, columns] = (mixed_ref[:, columns] * factor * gain_ref[:, columns]).astype(
            normed_ref.dtype
        )
    for d in range(seq_count):
        over(d).wait_send()
    for d in range(1, seq_count):
        away(d, me).wait_send()


def exchange(part, stream, gain):
    seq_count = part.shape[0]
    rows, features = part.shape[2:]
    whole = pl.BlockSpec(memory_space=pltpu.VMEM)
    return pl.pallas_call(
        functools.partial(exchange_kernel, seq_count),
        out_shape=(
            jax.ShapeDtypeStruct(stream.shape, jnp.float32),
            jax.ShapeDtypeStruct(stream.shape, jnp.bfloat16),
        ),
        in_specs=[whole] * 3,
        out_specs=(whole, whole),
        scratch_shapes=[pltpu.VMEM((seq_count, rows, features), part.dtype) for _ in range(3)]
        + [pltpu.SemaphoreType.DMA((seq_count,)) for _ in range(4)],
        compiler_params=pltpu.CompilerParams(
            collective_id=3, has_side_effects=True, vmem_limit_bytes=VMEM_LIMIT
        ),
        name="exchange",
    )(part, stream, gain)


def scatter_kernel(
    high, parts, part_ref, mixed_ref, out_ref, near, sums, across, running, line,
    near_s, near_r, across_s, across_r, line_s, line_r
):
    h, l, e = split_position()
    rows = part_ref.shape[-2] // parts
    mesh_id = pl.DeviceIdType.MESH
    order = []
    for i in range(high):
        order.append(i // 2 if i % 2 == 0 else high - 1 - i // 2)
    line_barrier(high, h, l, e)

    def to_near(h0, l0, c):
        at = pl.ds(c * rows, rows)
        return pltpu.make_async_remote_copy(
            src_ref=part_ref.at[h0, l0, 1 - e, at],
            dst_ref=near.at[h0, l0, at],
            send_sem=near_s.at[h0, l0, c],
            recv_sem=near_r.at[h0, l0, c],
            device_id={"exp": 1 - e},
            device_id_type=mesh_id,
        )

    def to_across(h0, c):
        at = pl.ds(c * rows, rows)
        return pltpu.make_async_remote_copy(
            src_ref=sums.at[h0, at],
            dst_ref=across.at[h0, at],
            send_sem=across_s.at[h0, c],
            recv_sem=across_r.at[h0, c],
            device_id={"seq": h * LOW + 1 - l},
            device_id_type=mesh_id,
        )

    def to_line(way, h0, c):
        at = pl.ds(c * rows, rows)
        return pltpu.make_async_remote_copy(
            src_ref=running.at[h0, at],
            dst_ref=line.at[way, h0, at],
            send_sem=line_s.at[way, h0, c],
            recv_sem=line_r.at[way, h0, c],
            device_id={"seq": (h - 1 + 2 * way) * LOW + l},
            device_id_type=mesh_id,
        )

    pieces = [(h0, c) for h0 in order for c in range(parts)]
    for h0, c in pieces:
        to_near(h0, 1 - l, c).start()
    for h0, c in pieces:
        to_near(h0, l, c).start()
    for h0, c in pieces:
        at = pl.ds(c * rows, rows)
        to_near(h0, 1 - l, c).wait_recv()
        value = part_ref[h0, 1 - l, e, at].astype(jnp.float32) + near[h0, 1 - l, at].astype(jnp.float32)
        sums[h0, at] = value.astype(sums.dtype)
        to_across(h0, c).start()
    for h0, c in pieces:
        at = pl.ds(c * rows, rows)
        to_near(h0, l, c).wait_recv()
        to_across(h0, c).wait_recv()

        def held():
            value = part_ref[h0, l, e, at].astype(jnp.float32) + near[h0, l, at].astype(jnp.float32)
            return value + across[h0, at].astype(jnp.float32)

        @pl.when(h0 < h)
        def _():
            @pl.when(h + 1 < high)
            def _():
                to_line(0, h0, c).wait_recv()
                running[h0, at] = (held() + line[0, h0, at].astype(jnp.float32)).astype(running.dtype)

            @pl.when(h + 1 >= high)
            def _():
                running[h0, at] = held().astype(running.dtype)

            to_line(0, h0, c).start()

        @pl.when(h0 > h)
        def _():
            @pl.when(h > 0)
            def _():
                to_line(1, h0, c).wait_recv()
                running[h0, at] = (held() + line[1, h0, at].astype(jnp.float32)).astype(running.dtype)

            @pl.when(h <= 0)
            def _():
                running[h0, at] = held().astype(running.dtype)

            to_line(1, h0, c).start()
    for c in range(parts):
        at = pl.ds(c * rows, rows)
        value = part_ref[h, l, e, at].astype(jnp.float32) + near[h, l, at].astype(jnp.float32)
        value = value + across[h, at].astype(jnp.float32) + mixed_ref[at, :]
        mixed_ref_sum = value

        @pl.when(h + 1 < high)
        def _():
            to_line(0, h, c).wait_recv()

        @pl.when(h + 1 >= high)
        def _():
            line[0, h, at] = jnp.zeros_like(line[0, h, at])

        @pl.when(h > 0)
        def _():
            to_line(1, h, c).wait_recv()

        @pl.when(h <= 0)
        def _():
            line[1, h, at] = jnp.zeros_like(line[1, h, at])

        value = mixed_ref_sum + line[0, h, at].astype(jnp.float32) + line[1, h, at].astype(jnp.float32)
        out_ref[at, :] = value.astype(out_ref.dtype)
    for h0, c in pieces:
        to_near(h0, l, c).wait_send()
        to_near(h0, 1 - l, c).wait_send()
        to_across(h0, c).wait_send()

        @pl.when(h0 < h)
        def _():
            to_line(0, h0, c).wait_send()

        @pl.when(h0 > h)
        def _():
            to_line(1, h0, c).wait_send()


def scatter(part, mixed, high):
    rows, width = mixed.shape
    parts = PARTS
    whole = pl.BlockSpec(memory_space=pltpu.VMEM)
    kind = part.dtype
    return pl.pallas_call(
        functools.partial(scatter_kernel, high, parts),
        out_shape=jax.ShapeDtypeStruct((rows, width), jnp.bfloat16),
        in_specs=[whole] * 2,
        out_specs=whole,
        scratch_shapes=[
            pltpu.VMEM((high, LOW, rows, width), kind),
            pltpu.VMEM((high, rows, width), kind),
            pltpu.VMEM((high, rows, width), kind),
            pltpu.VMEM((high, rows, width), kind),
            pltpu.VMEM((2, high, rows, width), kind),
        ]
        + [pltpu.SemaphoreType.DMA((high, LOW, parts))] * 2
        + [pltpu.SemaphoreType.DMA((high, parts))] * 2
        + [pltpu.SemaphoreType.DMA((2, high, parts))] * 2,
        compiler_params=pltpu.CompilerParams(
            collective_id=5, has_side_effects=True, vmem_limit_bytes=VMEM_LIMIT
        ),
        name="scatter",
    )(part, mixed)


def attend(queries, keys, values, query_start):
    rows = queries.shape[0]
    groups = keys.shape[1] // HD
    per_group = queries.shape[1] // (groups * HD)
    query_group = queries.reshape(rows, groups, per_group, HD)
    keyed = keys.reshape(-1, groups, HD)
    valued = values.reshape(-1, groups, HD)
    scores = jnp.einsum(
        "tghd,sgd->gths", query_group, keyed, preferred_element_type=jnp.float32
    ) / jnp.sqrt(jnp.float32(HD))
    query_pos = query_start + jnp.arange(rows, dtype=jnp.int32)
    key_pos = jnp.arange(keyed.shape[0], dtype=jnp.int32)
    allowed = (key_pos[None, :] <= query_pos[:, None])[None, :, None, :]
    scores = jnp.where(allowed, scores, neg_large)
    exps = jnp.exp(scores - jnp.max(scores, axis=-1, keepdims=True))
    total = jnp.sum(exps, axis=-1)
    summed = jnp.einsum(
        "gths,sgd->gthd", exps.astype(jnp.bfloat16), valued, preferred_element_type=jnp.float32
    )
    return (summed / total[..., None]).transpose(1, 0, 2, 3).reshape(rows, -1).astype(jnp.bfloat16)


def attend_kernel(query_ref, kv_ref, out_ref):
    blocks, span, double = kv_ref.shape
    half = double // 2
    groups = half // HD
    rows = query_ref.shape[0]
    per_group = query_ref.shape[1] // (groups * HD)
    me = lax.axis_index("seq")
    scale = 1.0 / (HD ** 0.5)
    stacked = per_group * rows
    for g in range(groups):
        q = jnp.concatenate(
            [query_ref[:, pl.ds((g * per_group + i) * HD, HD)] for i in range(per_group)], axis=0
        )

        def piece(b, state, masked):
            largest, total, summed = state
            k = kv_ref[b, :, pl.ds(g * HD, HD)]
            v = kv_ref[b, :, pl.ds(half + g * HD, HD)]
            scores = lax.dot_general(
                q, k, (((1,), (1,)), ((), ())), preferred_element_type=jnp.float32
            ) * scale
            if masked:
                row = lax.broadcasted_iota(jnp.int32, scores.shape, 0) % rows
                column = lax.broadcasted_iota(jnp.int32, scores.shape, 1)
                scores = jnp.where(column <= row, scores, neg_large)
            new = jnp.maximum(largest, jnp.max(scores, axis=-1, keepdims=True))
            rescale = jnp.exp(largest - new)
            exps = jnp.exp(scores - new)
            total = total * rescale + jnp.sum(exps, axis=-1, keepdims=True)
            summed = summed * rescale + jnp.dot(
                exps.astype(jnp.bfloat16), v, preferred_element_type=jnp.float32
            )
            return new, total, summed

        state = (
            jnp.full((stacked, 1), neg_large, jnp.float32),
            jnp.zeros((stacked, 1), jnp.float32),
            jnp.zeros((stacked, HD), jnp.float32),
        )
        state = piece(me, state, True)
        state = lax.fori_loop(0, me, lambda b, s: piece(b, s, False), state)
        result = (state[2] / state[1]).astype(out_ref.dtype)
        for i in range(per_group):
            out_ref[:, pl.ds((g * per_group + i) * HD, HD)] = result[i * rows : (i + 1) * rows]


def attend_fast(queries, kv):
    whole = pl.BlockSpec(memory_space=pltpu.VMEM)
    return pl.pallas_call(
        attend_kernel,
        out_shape=jax.ShapeDtypeStruct(queries.shape, jnp.bfloat16),
        in_specs=[whole] * 2,
        out_specs=whole,
        compiler_params=pltpu.CompilerParams(vmem_limit_bytes=VMEM_LIMIT),
        name="attend",
    )(queries, kv)


def on_device(
    stream,
    queries,
    key_rows,
    value_rows,
    out_weight,
    norm_gain,
    expert_ids,
    gate_weights,
    expert_in,
    expert_out,
):
    seq_count = lax.axis_size("seq")
    exp_count = lax.axis_size("exp")
    high = seq_count // LOW
    span = queries.shape[0]
    local_rows, width = stream.shape
    top = expert_ids.shape[1]
    meta = jnp.concatenate([expert_ids.astype(jnp.float32), gate_weights], axis=1)
    meta = jnp.pad(meta, ((0, 0), (0, 128 - 2 * top)))
    kv = jnp.concatenate([key_rows, value_rows], axis=1)
    all_kv, all_meta = gather((kv, meta), (False, True), (1, 1), high, 1)
    all_kv = all_kv.reshape(seq_count, span, -1)
    context = attend_fast(queries, all_kv)
    (all_context,) = gather((context,), (False,), (PARTS,), high, 2)
    all_context = all_context.reshape(seq_count * span, -1)
    part = lax.dot_general(
        all_context, out_weight, (((1,), (1,)), ((), ())), preferred_element_type=jnp.float32
    ).astype(jnp.bfloat16)
    part = part.reshape(seq_count, exp_count, local_rows, -1)
    mixed, normed = exchange(part, stream, norm_gain.reshape(1, -1))
    (all_normed,) = gather((normed,), (True,), (PARTS,), high, 4)
    blocks = seq_count * exp_count
    all_normed = all_normed.reshape(blocks, local_rows, width)
    local_experts = expert_in.shape[0]
    hidden_units = expert_out.shape[1]
    device = lax.axis_index("seq") * exp_count + lax.axis_index("exp")
    all_meta = all_meta.reshape(blocks, local_rows, -1)
    ids = all_meta[..., :top].astype(jnp.int32)
    gates = all_meta[..., top : 2 * top]
    here = device * local_experts + jnp.arange(local_experts, dtype=jnp.int32)
    hit = ids[:, None, :, :] == here[None, :, None, None]
    chosen = jnp.any(hit, axis=-1)
    gate = jnp.sum(jnp.where(hit, gates[:, None], 0.0), axis=-1)
    place = jnp.cumsum(chosen.astype(jnp.int32), axis=-1) - 1
    onehot = chosen[:, :, None, :] & (
        place[:, :, None, :] == jnp.arange(CAP, dtype=jnp.int32)[None, None, :, None]
    )
    slot_gate = jnp.sum(jnp.where(onehot, gate[:, :, None, :], 0.0), axis=-1)
    chooser = onehot.astype(jnp.bfloat16).reshape(blocks, local_experts * CAP, local_rows)
    arranged = (
        jnp.einsum("bsr,brd->bsd", chooser, all_normed, preferred_element_type=jnp.float32)
        .astype(jnp.bfloat16)
        .reshape(blocks, local_experts, CAP, width)
    )
    gate_up = jnp.einsum("secd,edf->secf", arranged, expert_in, preferred_element_type=jnp.float32)
    act = (jax.nn.silu(gate_up[..., :hidden_units]) * gate_up[..., hidden_units:]).astype(
        jnp.bfloat16
    )
    result = jnp.einsum("secf,efd->secd", act, expert_out, preferred_element_type=jnp.float32)
    result = (result * slot_gate[..., None]).astype(jnp.bfloat16)
    partial = jnp.einsum(
        "bsr,bsd->brd",
        chooser,
        result.reshape(blocks, local_experts * CAP, width),
        preferred_element_type=jnp.float32,
    ).astype(jnp.bfloat16)
    partial = partial.reshape(high, LOW, exp_count, local_rows, width)
    return scatter(partial, mixed, high)


def solution(mesh):
    in_specs = (
        P(("groups", "seq", "exp"), None),
        P(("groups", "seq"), "exp"),
        P(("groups", "seq"), "exp"),
        P(("groups", "seq"), "exp"),
        P("seq", "exp"),
        P(),
        P(("groups", "seq", "exp"), None),
        P(("groups", "seq", "exp"), None),
        P(("seq", "exp"), None, None),
        P(("seq", "exp"), None, None),
    )
    out_specs = P(("groups", "seq", "exp"), None)
    return jax.shard_map(
        on_device, mesh=mesh, in_specs=in_specs, out_specs=out_specs, check_vma=False
    )
```

time: 393 us -> 213 us (0.54); the launches traced: 387 us -> 212 us
  Pallas kernels: 0 us -> 169 us
  blocking collectives: 151 us -> 0 us
  waiting for transfers between devices: 118 us -> 0 us
  local copies, waits for them, and re-layouts: 40.3 us -> 5.96 us
  between operations: 13.6 us -> 0.14 us
  other arithmetic: 16.9 us -> 4.57 us
  matrix products: 40.9 us -> 32.4 us
  starting transfers between devices: 5.77 us -> 0 us
    pallas_call x0 -> x6, Pallas kernels: none -> 169 us  [the longest x3 111 us: gather(): pl.pallas_call(functools.partial(gather_kernel, high, cross, parts), out_...]
    all_to_all x3 -> x0, blocking collectives: 87.6 us -> none  [the longest x1 75 us: on_device(): lax.all_to_all(sectioned, 'seq', split_axis=0, concat_axis=0, tiled=True)]
    all_to_all x1 -> x0, waiting for transfers between devices: 67.8 us -> none  [on_device(): lax.all_to_all(finished, 'seq', split_axis=0, concat_axis=0, tiled=True)]
    all_gather x2 -> x0, blocking collectives: 63.9 us -> none  [the longest x1 34 us: on_device(): value_piece = lax.all_gather(value_rows, 'seq', axis=0, tiled=True)]
    all_gather x1 -> x0, waiting for transfers between devices: 45.5 us -> none  [on_device(): lax.all_gather(out_weight, 'seq', axis=0, tiled=True)]
    another operation x6 -> x0, local copies, waits for them, and re-layouts: 20.4 us -> none  [the longest x2 7.57 us: on_device(): outgoing.reshape(seq_count, exp_count, local_experts, CAP, width)]
    all_to_all x4 -> x0, local copies, waits for them, and re-layouts: 12.1 us -> none  [the longest x1 4.95 us: on_device(): lax.all_to_all(lax.all_to_all(sectioned, 'seq', split_axis=0, concat_axis...]
    reduce_sum x6 -> x2, other arithmetic: 12.3 us -> 0.36 us  [the longest x1 0.18 us: on_device(): slot_gate = jnp.sum(jnp.where(onehot, gate[:, :, None, :], 0.0), axis=-1)]
  transfers between devices with their start and end apart: 3 -> 0, of which waited for: 3 -> 0; matrix products, arithmetic and copies ran while one was open for 7% -> 0% of each run, Pallas kernels for 0% -> 0%
where the time goes in v1:
time: 213 us; the launch traced here: 212 us
  Pallas kernels  169 us (79%)
  matrix products  32.4 us (15%)
  local copies, waits for them, and re-layouts  5.96 us (3%)
  other arithmetic  4.57 us (2%)
    pallas_call x3, Pallas kernels, gather(): pl.pallas_call(functools.partial(gather_kernel, high, cross, parts), out_...  111 us
    pallas_call x1, Pallas kernels, scatter(): pl.pallas_call(functools.partial(scatter_kernel, high, parts), out_shape=...  38.6 us
    dot_general x1, matrix products, on_device(): jnp.einsum('secd,edf->secf', arranged, expert_in, preferred_element_type=...  10.8 us
    pallas_call x1, Pallas kernels, exchange(): pl.pallas_call(functools.partial(exchange_kernel, seq_count), out_shape=(...  10.4 us
    pallas_call x1, Pallas kernels, attend_fast(): pl.pallas_call(attend_kernel, out_shape=jax.ShapeDtypeStruct(queries.shap...  9.5 us
    dot_general x1, matrix products, on_device(): jnp.einsum('secf,efd->secd', act, expert_out, preferred_element_type=jnp....  7.71 us
    dot_general x1, matrix products, on_device(): jnp.einsum('bsr,bsd->brd', chooser, result.reshape(blocks, local_experts...  6.36 us
    dot_general x1, matrix products, on_device(): lax.dot_general(all_context, out_weight, (((1,), (1,)), ((), ())), prefer...  4.3 us

profile of v1, /device:TPU:16, one launch (start us, length us, event | category | flops | bytes accessed | tf_op | source)
XLA Modules:
  0.0 212.3 jit_solution(17587628509631543750)
XLA Ops:
  0.0 0.0 copy-start
  0.0 0.1 eq.43
  0.1 0.8 convert_element_type.31
  0.9 0.7 pad_maximum_fusion.1
  1.6 0.1 copy.38
  1.6 0.6 pad.4.refs_1_
  2.2 1.5 pad_maximum_fusion.refs_0_
  3.8 21.6 %gather1.1 = (bf16[4,2,128,512]{3,2,1,0:T(8,128)(2,1)}, f32[4,2,2,64,128]{4,3,2,1,0:T(8,128)}) custom-call(bf16[128,512]{1,0:T(8,128)(2,1)} %pad_maximum_fusion.refs_0_, f32[64,128]{1,0:T(8,128)} %pad.4.refs_1_), custom_call_target="tpu_custom_call" | custom-call | tf_op jit(solution)/shard_map/gather1/pallas_call | solution.py:160
  25.4 9.5 %attend.1.refs_0_ = bf16[128,2048]{1,0:T(8,128)(2,1)} custom-call(bf16[128,2048]{1,0:T(8,128)(2,1)} %query_ref.1, bf16[8,128,512]{2,1,0:T(8,128)(2,1)} %bitcast.45), custom_call_target="tpu_custom_call" | custom-call | tf_op jit(solution)/shard_map/attend/pallas_call | solution.py:489
  34.9 1.4 fusion.20
  36.3 0.2 copy.50
  36.5 0.2 compare_reduce_fusion
  36.6 0.9 reduce_window_sum.11
  37.6 0.2 copy.44
  37.7 0.2 fusion.18
  37.9 0.2 select_reduce_fusion
  38.1 0.1 fusion.15
  38.3 56.3 %gather2.1 = bf16[4,2,128,2048]{3,2,1,0:T(8,128)(2,1)} custom-call(bf16[128,2048]{1,0:T(8,128)(2,1)} %attend.1.refs_0_), custom_call_target="tpu_custom_call" | custom-call | tf_op jit(solution)/shard_map/gather2/pallas_call | solution.py:160
  94.6 0.0 copy-done
  94.6 4.3 %convolution_convert_fusion.2 = bf16[1024,256]{1,0:T(8,128)(2,1)} fusion(bf16[1024,2048]{1,0:T(8,128)(2,1)} %bitcast.42, bf16[256,2048]{1,0:T(8,128)(2,1)S(1)} %copy-done), kind=kOutput, calls=%fused_computation.12 | convolution fusion | flops 1074003968 | bytes 5767168 | tf_op jit(solution)/shard_map/dot_general | solution.py:525
  98.9 10.4 %exchange.1 = (f32[64,2048]{1,0:T(8,128)}, bf16[64,2048]{1,0:T(8,128)(2,1)}) custom-call(bf16[8,2,64,256]{3,2,1,0:T(8,128)(2,1)} %bitcast.46, bf16[64,2048]{1,0:T(8,128)(2,1)} %stream_ref.1, f32[1,2048]{1,0:T(1,128)} %bitcast.47), custom_call_target="tpu_custom_call" | custom-call | tf_op jit(solution)/shard_map/exchange/pallas_call | solution.py:247
  109.3 32.8 %gather4.1 = bf16[4,2,2,64,2048]{4,3,2,1,0:T(8,128)(2,1)} custom-call(bf16[64,2048]{1,0:T(8,128)(2,1)} %get-tuple-element.11.refs_0_), custom_call_target="tpu_custom_call" | custom-call | tf_op jit(solution)/shard_map/gather4/pallas_call | solution.py:160
  142.1 3.2 %convolution_convert_fusion.1 = bf16[16,48,2048]{2,1,0:T(8,128)(2,1)S(1)} fusion(bf16[16,64,2048]{2,1,0:T(8,128)(2,1)} %bitcast.41, pred[16,48,64]{2,0,1:T(8,128)(4,1)S(1)} %fusion.15), kind=kOutput, calls=%fused_computation.8 | convolution fusion | flops 202899456 | bytes 7389184 | tf_op jit(solution)/shard_map/bsr,brd->bsd/dot_general | solution.py:550
  145.3 1.7 copy.43
  147.0 10.8 %fusion.7 = f32[16,4,12,1536]{3,0,2,1:T(8,128)S(1)} fusion(bf16[16,4,12,2048]{3,0,2,1:T(8,128)(2,1)S(1)} %bitcast.39, bf16[4,2048,1536]{2,1,0:T(8,128)(2,1)} %param.18), kind=kOutput, calls=%fused_computation.6 | convolution fusion | flops 4831838208 | bytes 33030144 | tf_op jit(solution)/shard_map/secd,edf->secf/dot_general | solution.py:554
  157.9 7.7 %fusion.4 = bf16[16,4,12,2048]{3,0,2,1:T(8,128)(2,1)S(1)} fusion(bf16[4,768,2048]{2,1,0:T(8,128)(2,1)} %param.19, f32[16,4,12]{0,2,1:T(8,128)S(1)} %select_reduce_fusion, f32[16,4,12,1536]{3,0,2,1:T(8,128)S(1)} %fusion.7), kind=kOutput, calls=%fused_computation.5 | convolution fusion | flops 2422603776 | bytes 20450304 | tf_op jit(solution)/shard_map/secf,efd->secd/dot_general | solution.py:558
  165.6 0.0 copy-start.1
  165.6 6.4 %convolution_convert_fusion = bf16[16,64,2048]{2,1,0:T(8,128)(2,1)} fusion(bf16[16,48,2048]{2,0,1:T(8,128)(2,1)S(1)} %bitcast.43, pred[16,48,64]{2,0,1:T(8,128)(4,1)S(1)} %fusion.15), kind=kOutput, calls=%fused_computation.7 | convolution fusion | flops 203423744 | bytes 7389184 | tf_op jit(solution)/shard_map/bsr,bsd->brd/dot_general | solution.py:560
  172.0 38.6 %scatter.1 = bf16[64,2048]{1,0:T(8,128)(2,1)} custom-call(bf16[4,2,2,64,2048]{4,3,2,1,0:T(8,128)(2,1)} %bitcast.40, f32[64,2048]{1,0:T(8,128)} %get-tuple-element.12.mixed_ref), custom_call_target="tpu_custom_call" | custom-call | tf_op jit(solution)/shard_map/scatter/pallas_call | solution.py:397
  210.6 1.7 copy.60
  212.3 0.0 copy-done.1
  (6 shorter events, 0.0 us)
Async XLA Ops:
  0.0 94.6 %copy-start = (bf16[256,2048]{1,0:T(8,128)(2,1)S(1)}, bf16[256,2048]{1,0:T(8,128)(2,1)}, u32[]{:S(2)}) copy-start(bf16[256,2048]{1,0:T(8,128)(2,1)} %param.14) | copy-start | bytes 3145732
  165.6 46.7 %copy-start.1 = (bf16[256,2048]{1,0:T(8,128)(2,1)S(1)}, bf16[256,2048]{1,0:T(8,128)(2,1)}, u32[]{:S(2)}) copy-start(bf16[256,2048]{1,0:T(8,128)(2,1)} %param.14) | copy-start | bytes 3145732

commit v2 on v1

v2 whole, which is shorter than its diff:
```python
import functools

import jax
import jax.numpy as jnp
from jax import lax
from jax.experimental import pallas as pl
from jax.experimental.pallas import tpu as pltpu
from jax.sharding import PartitionSpec as P

HD = 128
EXPERTS = 64
CAP = 12
LOW = 2
PARTS = 2
VMEM_LIMIT = 67043328
neg_large = -1e30


def split_position():
    seq = lax.axis_index("seq")
    return seq // LOW, seq % LOW, lax.axis_index("exp")


def line_barrier(high, h, l, e):
    barrier = pltpu.get_barrier_semaphore()

    def greet(target):
        pl.semaphore_signal(barrier, inc=1, device_id=target, device_id_type=pl.DeviceIdType.MESH)

    @pl.when(h + 1 < high)
    def _():
        greet({"seq": (h + 1) * LOW + l})

    @pl.when(h > 0)
    def _():
        greet({"seq": (h - 1) * LOW + l})

    greet({"seq": h * LOW + 1 - l})
    greet({"exp": 1 - e})

    ends = jnp.where(h + 1 < high, 1, 0) + jnp.where(h > 0, 1, 0)
    pl.semaphore_wait(barrier, ends + 2)


def gather_steps(high, outs, cross, parts, recv, send, h, l, e):
    count = len(outs)

    def slot(a, h0, l0, e0, c):
        rows = outs[a].shape[-2] // parts[a]
        at = (h0, l0, e0) if cross[a] else (h0, l0)
        return outs[a].at[at + (pl.ds(c * rows, rows),)]

    def copy(a, h0, l0, e0, c, way):
        target = (
            {"seq": (h + 1) * LOW + l},
            {"seq": (h - 1) * LOW + l},
            {"seq": h * LOW + 1 - l},
            {"exp": 1 - e},
        )[way]
        ref = slot(a, h0, l0, e0, c)
        return pltpu.make_async_remote_copy(
            src_ref=ref,
            dst_ref=ref,
            send_sem=send[a].at[way, h0, l0, c],
            recv_sem=recv[a].at[h0, l0, e0, c],
            device_id=target,
            device_id_type=pl.DeviceIdType.MESH,
        )

    def pass_on(a, h0, c, right, left):
        if right:
            @pl.when(h + 1 < high)
            def _():
                copy(a, h0, l, e, c, 0).start()
        if left:
            @pl.when(h > 0)
            def _():
                copy(a, h0, l, e, c, 1).start()
        copy(a, h0, l, e, c, 2).start()
        if cross[a]:
            copy(a, h0, l, e, c, 3).start()

    def from_across(a, h0, c):
        copy(a, h0, 1 - l, e, c, 2).wait_recv()
        if cross[a]:
            copy(a, h0, 1 - l, e, c, 3).start()

    for a in range(count):
        for c in range(parts[a]):
            pass_on(a, h, c, True, True)
    for t in range(1, high + 1):
        if t < high:
            for a in range(count):
                for c in range(parts[a]):
                    @pl.when(h - t >= 0)
                    def _():
                        copy(a, h - t, l, e, c, 0).wait_recv()
                        pass_on(a, h - t, c, True, False)

                    @pl.when(h + t < high)
                    def _():
                        copy(a, h + t, l, e, c, 1).wait_recv()
                        pass_on(a, h + t, c, False, True)
        for a in range(count):
            for c in range(parts[a]):
                if t == 1:
                    from_across(a, h, c)
                else:
                    @pl.when(h - t + 1 >= 0)
                    def _():
                        from_across(a, h - t + 1, c)

                    @pl.when(h + t - 1 < high)
                    def _():
                        from_across(a, h + t - 1, c)
    for a in range(count):
        for c in range(parts[a]):
            for h0 in range(high):
                if cross[a]:
                    for l0 in range(LOW):
                        copy(a, h0, l0, 1 - e, c, 3).wait_recv()
                        copy(a, h0, l0, e, c, 3).wait_send()
                copy(a, h0, l, e, c, 2).wait_send()

                @pl.when((h + 1 < high) & (h0 <= h))
                def _():
                    copy(a, h0, l, e, c, 0).wait_send()

                @pl.when((h > 0) & (h0 >= h))
                def _():
                    copy(a, h0, l, e, c, 1).wait_send()


def all_barrier(high, h, l, e):
    barrier = pltpu.get_barrier_semaphore()
    mesh_id = pl.DeviceIdType.MESH
    for d in range(1, high):
        pl.semaphore_signal(
            barrier, inc=1, device_id={"seq": (h + d) % high * LOW + l}, device_id_type=mesh_id
        )
    pl.semaphore_signal(barrier, inc=1, device_id={"seq": h * LOW + 1 - l}, device_id_type=mesh_id)
    pl.semaphore_signal(barrier, inc=1, device_id={"exp": 1 - e}, device_id_type=mesh_id)
    pl.semaphore_wait(barrier, high + 1)


def attend(query_ref, kv_ref, out_ref, me):
    half = kv_ref.shape[-1] // 2
    groups = half // HD
    rows, columns = query_ref.shape
    per_group = columns // (groups * HD)
    scale = 1.0 / (HD ** 0.5)
    stacked = per_group * rows
    for g in range(groups):
        q = jnp.concatenate(
            [query_ref[:, pl.ds((g * per_group + i) * HD, HD)] for i in range(per_group)], axis=0
        )

        def piece(b, state, masked):
            largest, total, summed = state
            k = kv_ref[b // LOW, b % LOW, :, pl.ds(g * HD, HD)]
            v = kv_ref[b // LOW, b % LOW, :, pl.ds(half + g * HD, HD)]
            scores = lax.dot_general(
                q, k, (((1,), (1,)), ((), ())), preferred_element_type=jnp.float32
            ) * scale
            if masked:
                row = lax.broadcasted_iota(jnp.int32, scores.shape, 0) % rows
                column = lax.broadcasted_iota(jnp.int32, scores.shape, 1)
                scores = jnp.where(column <= row, scores, neg_large)
            new = jnp.maximum(largest, jnp.max(scores, axis=-1, keepdims=True))
            rescale = jnp.exp(largest - new)
            exps = jnp.exp(scores - new)
            total = total * rescale + jnp.sum(exps, axis=-1, keepdims=True)
            summed = summed * rescale + jnp.dot(
                exps.astype(jnp.bfloat16), v, preferred_element_type=jnp.float32
            )
            return new, total, summed

        state = (
            jnp.full((stacked, 1), neg_large, jnp.float32),
            jnp.zeros((stacked, 1), jnp.float32),
            jnp.zeros((stacked, HD), jnp.float32),
        )
        state = piece(me, state, True)
        state = lax.fori_loop(0, me, lambda b, s: piece(b, s, False), state)
        result = (state[2] / state[1]).astype(out_ref.dtype)
        for i in range(per_group):
            out_ref[:, pl.ds((g * per_group + i) * HD, HD)] = result[i * rows : (i + 1) * rows]


def front_kernel(
    high, kv_in, meta_in, query_ref, weight_in, stream_ref, gain_ref,
    mixed_ref, normed_ref, meta_all,
    kv_all, weights, context, contexts, part, mine, ready, landed,
    kv_r, meta_r, kv_s, meta_s, local, weight_sem, line_s, line_r, over_s, over_r, away_s, away_r
):
    h, l, e = split_position()
    mesh_id = pl.DeviceIdType.MESH
    copies = [
        pltpu.make_async_copy(kv_in, kv_all.at[h, l], local.at[0]),
        pltpu.make_async_copy(meta_in, meta_all.at[h, l, e], local.at[1]),
        pltpu.make_async_copy(weight_in, weights.at[l], local.at[2]),
    ]
    for one in copies:
        one.start()
    all_barrier(high, h, l, e)
    for one in copies:
        one.wait()
    gather_steps(
        high, (kv_all, meta_all), (False, True), (1, 1), (kv_r, meta_r), (kv_s, meta_s), h, l, e
    )
    weight_copy = pltpu.make_async_remote_copy(
        src_ref=weights.at[l],
        dst_ref=weights.at[l],
        send_sem=weight_sem.at[0],
        recv_sem=weight_sem.at[1],
        device_id={"seq": h * LOW + 1 - l},
        device_id_type=mesh_id,
    )
    weight_copy.start()
    attend(query_ref, kv_all, context, h * LOW + l)
    own = pltpu.make_async_copy(context, contexts.at[h], local.at[0])
    own.start()
    own.wait()
    parts = PARTS
    rows = context.shape[0] // parts

    def hop(way, h0, c):
        ref = contexts.at[h0, pl.ds(c * rows, rows)]
        return pltpu.make_async_remote_copy(
            src_ref=ref,
            dst_ref=ref,
            send_sem=line_s.at[way, h0, c],
            recv_sem=line_r.at[h0, c],
            device_id={"seq": (h + 1 - 2 * way) * LOW + l},
            device_id_type=mesh_id,
        )

    def hops(h0, c, right, left):
        if right:
            @pl.when(h + 1 < high)
            def _():
                hop(0, h0, c).start()
        if left:
            @pl.when(h > 0)
            def _():
                hop(1, h0, c).start()

    for c in range(parts):
        hops(h, c, True, True)
    for t in range(1, high):
        for c in range(parts):
            @pl.when(h - t >= 0)
            def _():
                hop(0, h - t, c).wait_recv()
                hops(h - t, c, True, False)

            @pl.when(h + t < high)
            def _():
                hop(1, h + t, c).wait_recv()
                hops(h + t, c, False, True)
    weight_back = pltpu.make_async_remote_copy(
        src_ref=weights.at[1 - l],
        dst_ref=weights.at[1 - l],
        send_sem=weight_sem.at[0],
        recv_sem=weight_sem.at[1],
        device_id={"seq": h * LOW + 1 - l},
        device_id_type=mesh_id,
    )
    weight_back.wait_recv()
    rows_e, features = part.shape[2:]
    slim = features // LOW

    def over(h0):
        return pltpu.make_async_remote_copy(
            src_ref=part.at[h0, 1 - e],
            dst_ref=mine.at[h0],
            send_sem=over_s.at[h0],
            recv_sem=over_r.at[h0],
            device_id={"exp": 1 - e},
            device_id_type=mesh_id,
        )

    def away(h0, source):
        return pltpu.make_async_remote_copy(
            src_ref=ready.at[h0],
            dst_ref=landed.at[source],
            send_sem=away_s.at[h0],
            recv_sem=away_r.at[source],
            device_id={"seq": h0 * LOW + l},
            device_id_type=mesh_id,
        )

    @pl.loop(0, high)
    def _(d):
        h0 = (h + 1 + d) % high
        for l0 in range(LOW):
            product = lax.dot_general(
                contexts[h0], weights[l0], (((1,), (1,)), ((), ())), preferred_element_type=jnp.float32
            ).astype(part.dtype)
            for e0 in range(2):
                part[h0, e0, :, pl.ds(l0 * slim, slim)] = product[e0 * rows_e : (e0 + 1) * rows_e]
        over(h0).start()

    for d in range(1, high + 1):
        h0 = (h + d) % high
        over(h0).wait_recv()
        total = part[h0, e].astype(jnp.float32) + mine[h0].astype(jnp.float32)
        ready[h0] = total.astype(ready.dtype)
        if d < high:
            away(h0, h).start()
    landed[h] = ready[h]
    for d in range(1, high):
        away((h + d) % high, (h + high - d) % high).wait_recv()
    squares = None
    for h0 in range(high):
        columns = pl.ds(h0 * features, features)
        value = stream_ref[:, columns].astype(jnp.float32) + landed[h0].astype(jnp.float32)
        mixed_ref[:, columns] = value
        term = jnp.sum(value * value, axis=-1, keepdims=True)
        squares = term if squares is None else squares + term
    factor = lax.rsqrt(squares / (high * features) + 1e-06)
    for h0 in range(high):
        columns = pl.ds(h0 * features, features)
        normed_ref[:, columns] = (mixed_ref[:, columns] * factor * gain_ref[:, columns]).astype(
            normed_ref.dtype
        )
    weight_copy.wait_send()
    for h0 in range(high):
        over(h0).wait_send()
        for c in range(parts):
            @pl.when((h + 1 < high) & (h0 <= h))
            def _():
                hop(0, h0, c).wait_send()

            @pl.when((h > 0) & (h0 >= h))
            def _():
                hop(1, h0, c).wait_send()
    for d in range(1, high):
        away((h + d) % high, h).wait_send()


def front(kv, meta, queries, weight, stream, gain, high):
    whole = pl.BlockSpec(memory_space=pltpu.VMEM)
    span = queries.shape[0]
    rows = stream.shape[0]
    features = weight.shape[0] * LOW
    kind = jnp.bfloat16
    sem = pltpu.SemaphoreType.DMA
    return pl.pallas_call(
        functools.partial(front_kernel, high),
        out_shape=(
            jax.ShapeDtypeStruct(stream.shape, jnp.float32),
            jax.ShapeDtypeStruct(stream.shape, kind),
            jax.ShapeDtypeStruct((high, LOW, 2) + meta.shape, meta.dtype),
        ),
        in_specs=[whole] * 6,
        out_specs=(whole,) * 3,
        scratch_shapes=[
            pltpu.VMEM((high, LOW) + kv.shape, kind),
            pltpu.VMEM((LOW,) + weight.shape, kind),
            pltpu.VMEM(queries.shape, kind),
            pltpu.VMEM((high,) + queries.shape, kind),
            pltpu.VMEM((high, 2, rows, features), kind),
            pltpu.VMEM((high, rows, features), kind),
            pltpu.VMEM((high, rows, features), kind),
            pltpu.VMEM((high, rows, features), kind),
            sem((high, LOW, 2, 1)),
            sem((high, LOW, 2, 1)),
            sem((4, high, LOW, 1)),
            sem((4, high, LOW, 1)),
            sem((3,)),
            sem((2,)),
            sem((2, high, PARTS)),
            sem((high, PARTS)),
            sem((high,)),
            sem((high,)),
            sem((high,)),
            sem((high,)),
        ],
        compiler_params=pltpu.CompilerParams(
            collective_id=1, has_side_effects=True, vmem_limit_bytes=VMEM_LIMIT
        ),
        name="front",
    )(kv, meta, queries, weight, stream, gain)


def back_kernel(
    high, parts, normed_ref, mixed_ref, choose_ref, combine_ref, first_hbm, second_hbm, out_ref,
    every, first, second, picked, act, near, sums, across, running, line,
    local, weight_sem, recv, send, near_s, near_r, across_s, across_r, line_s, line_r
):
    h, l, e = split_position()
    experts, width, double = first.shape
    hidden = double // 2
    slots = picked.shape[2]
    loads = []
    for i in range(experts):
        loads.append(pltpu.make_async_copy(first_hbm.at[i], first.at[i], weight_sem.at[0, i]))
        loads.append(pltpu.make_async_copy(second_hbm.at[i], second.at[i], weight_sem.at[1, i]))
    for one in loads:
        one.start()
    own = pltpu.make_async_copy(normed_ref, every.at[h, l, e], local.at[0])
    own.start()
    line_barrier(high, h, l, e)
    own.wait()
    gather_steps(high, (every,), (True,), (parts,), (recv,), (send,), h, l, e)
    for one in loads:
        one.wait()
    rows_all = every.shape[1] * every.shape[2] * every.shape[3]
    tile = 512

    @pl.loop(0, high)
    def _(h0):
        for n in range(0, width, tile):
            tokens = every[h0, :, :, :, pl.ds(n, tile)].reshape(rows_all, tile)
            value = jnp.dot(choose_ref[h0], tokens, preferred_element_type=jnp.float32)
            for i in range(experts):
                picked[i, h0, :, pl.ds(n, tile)] = value[i * slots : (i + 1) * slots].astype(
                    picked.dtype
                )

    def run(i, carry):
        step = 256
        rows = picked[i].reshape(high * slots, width)
        for f in range(0, hidden, step):
            gate = jnp.dot(rows, first[i, :, pl.ds(f, step)], preferred_element_type=jnp.float32)
            up = jnp.dot(
                rows, first[i, :, pl.ds(hidden + f, step)], preferred_element_type=jnp.float32
            )
            act[:, pl.ds(f, step)] = (gate / (1.0 + jnp.exp(-gate)) * up).astype(act.dtype)
        for n in range(0, width, tile):
            value = jnp.dot(
                act[...], second[i, :, pl.ds(n, tile)], preferred_element_type=jnp.float32
            ).astype(picked.dtype)
            picked[i, :, :, pl.ds(n, tile)] = value.reshape(high, slots, tile)
        return carry

    lax.fori_loop(0, experts, run, 0)
    scatter_steps(
        high, parts, every, mixed_ref, out_ref, near, sums, across, running, line,
        near_s, near_r, across_s, across_r, line_s, line_r, h, l, e, combine_ref, picked, tile
    )


def scatter_steps(
    high, parts, part_ref, mixed_ref, out_ref, near, sums, across, running, line,
    near_s, near_r, across_s, across_r, line_s, line_r, h, l, e, combine_ref, picked, tile
):
    rows = part_ref.shape[-2] // parts
    mesh_id = pl.DeviceIdType.MESH
    order = []
    for i in range(high):
        order.append(i // 2 if i % 2 == 0 else high - 1 - i // 2)

    def to_near(h0, l0, c):
        at = pl.ds(c * rows, rows)
        return pltpu.make_async_remote_copy(
            src_ref=part_ref.at[h0, l0, 1 - e, at],
            dst_ref=near.at[h0, l0, at],
            send_sem=near_s.at[h0, l0, c],
            recv_sem=near_r.at[h0, l0, c],
            device_id={"exp": 1 - e},
            device_id_type=mesh_id,
        )

    def to_across(h0, c):
        at = pl.ds(c * rows, rows)
        return pltpu.make_async_remote_copy(
            src_ref=sums.at[h0, at],
            dst_ref=across.at[h0, at],
            send_sem=across_s.at[h0, c],
            recv_sem=across_r.at[h0, c],
            device_id={"seq": h * LOW + 1 - l},
            device_id_type=mesh_id,
        )

    def to_line(way, h0, c):
        at = pl.ds(c * rows, rows)
        return pltpu.make_async_remote_copy(
            src_ref=running.at[h0, at],
            dst_ref=line.at[way, h0, at],
            send_sem=line_s.at[way, h0, c],
            recv_sem=line_r.at[way, h0, c],
            device_id={"seq": (h - 1 + 2 * way) * LOW + l},
            device_id_type=mesh_id,
        )

    pieces = [(h0, c) for h0 in order for c in range(parts)]
    experts, width = picked.shape[0], picked.shape[-1]
    shape = part_ref.shape[1:4]
    for h0 in order:
        for n in range(0, width, tile):
            rows_here = jnp.concatenate(
                [picked[i, h0, :, pl.ds(n, tile)] for i in range(experts)], axis=0
            )
            value = jnp.dot(combine_ref[h0], rows_here, preferred_element_type=jnp.float32)
            part_ref[h0, :, :, :, pl.ds(n, tile)] = value.astype(part_ref.dtype).reshape(
                shape + (tile,)
            )
        for c in range(parts):
            to_near(h0, 1 - l, c).start()
        for c in range(parts):
            to_near(h0, l, c).start()
    for h0, c in pieces:
        at = pl.ds(c * rows, rows)
        to_near(h0, 1 - l, c).wait_recv()
        value = part_ref[h0, 1 - l, e, at].astype(jnp.float32) + near[h0, 1 - l, at].astype(jnp.float32)
        sums[h0, at] = value.astype(sums.dtype)
        to_across(h0, c).start()
    for h0, c in pieces:
        at = pl.ds(c * rows, rows)
        to_near(h0, l, c).wait_recv()
        to_across(h0, c).wait_recv()

        def held():
            value = part_ref[h0, l, e, at].astype(jnp.float32) + near[h0, l, at].astype(jnp.float32)
            return value + across[h0, at].astype(jnp.float32)

        @pl.when(h0 < h)
        def _():
            @pl.when(h + 1 < high)
            def _():
                to_line(0, h0, c).wait_recv()
                running[h0, at] = (held() + line[0, h0, at].astype(jnp.float32)).astype(running.dtype)

            @pl.when(h + 1 >= high)
            def _():
                running[h0, at] = held().astype(running.dtype)

            to_line(0, h0, c).start()

        @pl.when(h0 > h)
        def _():
            @pl.when(h > 0)
            def _():
                to_line(1, h0, c).wait_recv()
                running[h0, at] = (held() + line[1, h0, at].astype(jnp.float32)).astype(running.dtype)

            @pl.when(h <= 0)
            def _():
                running[h0, at] = held().astype(running.dtype)

            to_line(1, h0, c).start()
    for c in range(parts):
        at = pl.ds(c * rows, rows)
        value = part_ref[h, l, e, at].astype(jnp.float32) + near[h, l, at].astype(jnp.float32)
        value = value + across[h, at].astype(jnp.float32) + mixed_ref[at, :]
        mixed_ref_sum = value

        @pl.when(h + 1 < high)
        def _():
            to_line(0, h, c).wait_recv()

        @pl.when(h + 1 >= high)
        def _():
            line[0, h, at] = jnp.zeros_like(line[0, h, at])

        @pl.when(h > 0)
        def _():
            to_line(1, h, c).wait_recv()

        @pl.when(h <= 0)
        def _():
            line[1, h, at] = jnp.zeros_like(line[1, h, at])

        value = mixed_ref_sum + line[0, h, at].astype(jnp.float32) + line[1, h, at].astype(jnp.float32)
        out_ref[at, :] = value.astype(out_ref.dtype)
    for h0, c in pieces:
        to_near(h0, l, c).wait_send()
        to_near(h0, 1 - l, c).wait_send()
        to_across(h0, c).wait_send()

        @pl.when(h0 < h)
        def _():
            to_line(0, h0, c).wait_send()

        @pl.when(h0 > h)
        def _():
            to_line(1, h0, c).wait_send()


def back(normed, mixed, choose, combine, expert_in, expert_out, high):
    rows, width = mixed.shape
    parts = PARTS
    whole = pl.BlockSpec(memory_space=pltpu.VMEM)
    away = pl.BlockSpec(memory_space=pl.ANY)
    kind = jnp.bfloat16
    sem = pltpu.SemaphoreType.DMA
    experts = expert_in.shape[0]
    slots = choose.shape[1] // experts
    return pl.pallas_call(
        functools.partial(back_kernel, high, parts),
        out_shape=jax.ShapeDtypeStruct((rows, width), kind),
        in_specs=[whole] * 4 + [away] * 2,
        out_specs=whole,
        scratch_shapes=[
            pltpu.VMEM((high, LOW, 2, rows, width), kind),
            pltpu.VMEM(expert_in.shape, kind),
            pltpu.VMEM(expert_out.shape, kind),
            pltpu.VMEM((experts, high, slots, width), kind),
            pltpu.VMEM((high * slots, expert_out.shape[1]), kind),
            pltpu.VMEM((high, LOW, rows, width), kind),
            pltpu.VMEM((high, rows, width), kind),
            pltpu.VMEM((high, rows, width), kind),
            pltpu.VMEM((high, rows, width), kind),
            pltpu.VMEM((2, high, rows, width), kind),
            sem((1,)),
            sem((2, experts)),
            sem((high, LOW, 2, parts)),
            sem((4, high, LOW, parts)),
        ]
        + [sem((high, LOW, parts))] * 2
        + [sem((high, parts))] * 2
        + [sem((2, high, parts))] * 2,
        compiler_params=pltpu.CompilerParams(
            collective_id=2, has_side_effects=True, vmem_limit_bytes=VMEM_LIMIT
        ),
        name="back",
    )(normed, mixed, choose, combine, expert_in, expert_out)


def on_device(
    stream,
    queries,
    key_rows,
    value_rows,
    out_weight,
    norm_gain,
    expert_ids,
    gate_weights,
    expert_in,
    expert_out,
):
    seq_count = lax.axis_size("seq")
    exp_count = lax.axis_size("exp")
    high = seq_count // LOW
    local_rows = stream.shape[0]
    top = expert_ids.shape[1]
    meta = jnp.concatenate([expert_ids.astype(jnp.float32), gate_weights], axis=1)
    meta = jnp.pad(meta, ((0, 0), (0, 128 - 2 * top)))
    kv = jnp.concatenate([key_rows, value_rows], axis=1)
    mixed, normed, all_meta = front(
        kv, meta, queries, out_weight, stream, norm_gain.reshape(1, -1), high
    )
    local_experts = expert_in.shape[0]
    device = lax.axis_index("seq") * exp_count + lax.axis_index("exp")
    inner = LOW * exp_count
    all_meta = all_meta.reshape(high * inner, local_rows, -1)
    ids = all_meta[..., :top].astype(jnp.int32)
    gates = all_meta[..., top : 2 * top]
    here = device * local_experts + jnp.arange(local_experts, dtype=jnp.int32)
    hit = ids[:, None, :, :] == here[None, :, None, None]
    chosen = jnp.any(hit, axis=-1)
    gate = jnp.sum(jnp.where(hit, gates[:, None], 0.0), axis=-1)
    place = jnp.cumsum(chosen.astype(jnp.int32), axis=-1) - 1
    place = jnp.where(chosen, place, -1).reshape(high, inner, local_experts, local_rows)
    gate = gate.reshape(high, inner, local_experts, local_rows)
    slot = jnp.arange(CAP, dtype=jnp.int32)
    same = jnp.eye(inner, dtype=jnp.bool_)
    choose = (
        (place.transpose(0, 2, 1, 3)[:, :, None, None, :, :] == slot[None, None, None, :, None, None])
        & same[None, None, :, None, :, None]
    ).astype(jnp.bfloat16)
    choose = choose.reshape(high, local_experts * inner * CAP, inner * local_rows)
    weigh = jnp.where(
        (place.transpose(0, 1, 3, 2)[:, :, :, :, None, None] == slot)
        & same[None, :, None, None, :, None],
        gate.transpose(0, 1, 3, 2)[:, :, :, :, None, None],
        0.0,
    ).astype(jnp.bfloat16)
    combine = weigh.reshape(high, inner * local_rows, local_experts * inner * CAP)
    return back(normed, mixed, choose, combine, expert_in, expert_out, high)


def solution(mesh):
    in_specs = (
        P(("groups", "seq", "exp"), None),
        P(("groups", "seq"), "exp"),
        P(("groups", "seq"), "exp"),
        P(("groups", "seq"), "exp"),
        P("seq", "exp"),
        P(),
        P(("groups", "seq", "exp"), None),
        P(("groups", "seq", "exp"), None),
        P(("seq", "exp"), None, None),
        P(("seq", "exp"), None, None),
    )
    out_specs = P(("groups", "seq", "exp"), None)
    return jax.shard_map(
        on_device, mesh=mesh, in_specs=in_specs, out_specs=out_specs, check_vma=False
    )
```

time: 213 us -> 169 us (0.79)
  matrix products: 32.4 us -> 0 us
  Pallas kernels: 169 us -> 151 us
  other arithmetic: 4.57 us -> 9.16 us
    dot_general x5 -> x0, matrix products: 32.4 us -> none  [the longest x1 10.8 us: on_device(): jnp.einsum('secd,edf->secf', arranged, expert_in, preferred_element_type=...]
    pallas_call x6 -> x2, Pallas kernels: 169 us -> 151 us  [the longest x1 77.2 us: front(): pl.pallas_call(functools.partial(front_kernel, high), out_shape=(jax.Shap...]
    another operation x1, other arithmetic: 0.9 us -> 3.79 us  [on_device(): place = jnp.cumsum(chosen.astype(jnp.int32), axis=-1) - 1]
    and x0 -> x10, local copies, waits for them, and re-layouts: none -> 2.89 us  [the longest x6 1.75 us: on_device(): (place.transpose(0, 1, 3, 2)[:, :, :, :, None, None] == slot) & same[None...]
where the time goes in v2:
time: 169 us; the launch traced here: 168 us
  Pallas kernels  151 us (89%)
  other arithmetic  9.16 us (5%)
  local copies, waits for them, and re-layouts  8.04 us (5%)
    pallas_call x1, Pallas kernels, front(): pl.pallas_call(functools.partial(front_kernel, high), out_shape=(jax.Shap...  77.2 us
    pallas_call x1, Pallas kernels, back(): pl.pallas_call(functools.partial(back_kernel, high, parts), out_shape=jax...  73.8 us
    another operation x1, other arithmetic, on_device(): place = jnp.cumsum(chosen.astype(jnp.int32), axis=-1) - 1  3.79 us

profile of v2, /device:TPU:16, one launch (start us, length us, event | category | flops | bytes accessed | tf_op | source)
XLA Modules:
  0.0 168.5 jit_solution(1541293580785866600)
XLA Ops:
  0.0 1.5 pad_maximum_fusion.kv_in
  1.5 0.7 convert_element_type.20
  2.2 0.7 pad_maximum_fusion.1
  2.9 0.1 copy.51
  3.0 0.6 pad.4.meta_in
  3.6 77.2 %front.1 = (f32[64,2048]{1,0:T(8,128)}, bf16[64,2048]{1,0:T(8,128)(2,1)}, f32[4,2,2,64,128]{4,3,2,1,0:T(8,128)}) custom-call(bf16[128,512]{1,0:T(8,128)(2,1)} %pad_maximum_fusion.kv_in, f32[64,128]{1,0:T(8,128)} %pad.4.meta_in, bf16[128,2048]{1,0:T(8,128)(2,1)} %query_ref.1, bf16[256,2048]{1,0:T(8,128)(2,1)} %weight_in.1, bf16[64,2048]{1,0:T(8,128)(2,1)} %stream_ref.1, ...), custom_call_target="tpu_custom_call" | custom-call | tf_op jit(solution)/shard_map/front/pallas_call | solution.py:349
  80.9 1.4 fusion.3
  82.3 0.2 copy.62
  82.5 0.2 compare_reduce_fusion
  82.7 3.8 %reduce_window_sum.11 = s32[4,4,4,64]{3,2,1,0:T(4,128)S(1)} reduce-window(s32[4,4,4,64]{3,2,1,0:T(4,128)S(1)} %convert_element_type.22, s32[]{:T(128)} %constant.24.clone.1), window={size=1x1x1x64 pad=0_0x0_0x0_0x63_0}, to_apply=%region_1.2 | reduce-window | flops 258048 | bytes 32772 | tf_op jit(solution)/shard_map/jit(cumsum)/reduce_window_sum | solution.py:655
  86.5 0.1 iota_compare_fusion
  86.6 0.3 and.48
  86.9 0.6 and.49
  87.4 0.4 copy.57
  87.9 0.2 copy.58
  88.1 0.2 fusion
  88.3 0.2 broadcast_in_dim.40
  88.5 0.5 broadcast_in_dim.41
  89.0 0.2 copy.61
  89.2 0.1 and.50
  89.3 0.2 and.51
  89.5 0.2 copy.56
  89.7 1.0 select_convert_fusion.combine_ref
  90.7 0.1 iota_compare_fusion.1
  90.8 0.3 and.42
  91.1 0.6 and.43
  91.7 0.1 copy.54
  91.8 0.1 and.44
  91.9 0.2 and.45
  92.1 0.8 and_convert_fusion.choose_ref
  93.0 73.8 %back.1 = bf16[64,2048]{1,0:T(8,128)(2,1)} custom-call(bf16[64,2048]{1,0:T(8,128)(2,1)} %get-tuple-element.8.normed_ref, f32[64,2048]{1,0:T(8,128)} %get-tuple-element.9.mixed_ref, bf16[4,192,256]{2,1,0:T(8,128)(2,1)} %and_convert_fusion.choose_ref, bf16[4,256,192]{2,1,0:T(8,128)(2,1)} %select_convert_fusion.combine_ref, bf16[4,2048,1536]{2,1,0:T(8,128)(2,1)} %first_hbm.1, ...), custom_call_target="tpu_custom_call" | custom-call | tf_op jit(solution)/shard_map/back/pallas_call | solution.py:591
  166.8 1.7 copy.64
  (9 shorter events, 0.1 us)

commit v3 on v2

--- a/solution.py
+++ b/solution.py
@@ -11,7 +11,7 @@
 EXPERTS = 64
 CAP = 12
 LOW = 2
-PARTS = 2
+PARTS = 4
 VMEM_LIMIT = 67043328
 neg_large = -1e30
 
@@ -42,7 +42,7 @@
     pl.semaphore_wait(barrier, ends + 2)
 
 
-def gather_steps(high, outs, cross, parts, recv, send, h, l, e):
+def gather_steps(high, outs, cross, parts, recv, send, h, l, e, beside=None):
     count = len(outs)
 
     def slot(a, h0, l0, e0, c):
@@ -88,6 +88,8 @@
     for a in range(count):
         for c in range(parts[a]):
             pass_on(a, h, c, True, True)
+    if beside is not None:
+        beside(0)
     for t in range(1, high + 1):
         if t < high:
             for a in range(count):
@@ -113,6 +115,8 @@
                     @pl.when(h + t - 1 < high)
                     def _():
                         from_across(a, h + t - 1, c)
+        if beside is not None and t < high:
+            beside(t)
     for a in range(count):
         for c in range(parts[a]):
             for h0 in range(high):
@@ -143,7 +147,7 @@
     pl.semaphore_wait(barrier, high + 1)
 
 
-def attend(query_ref, kv_ref, out_ref, me):
+def attend(query_ref, kv_ref, out_ref, me, done):
     half = kv_ref.shape[-1] // 2
     groups = half // HD
     rows, columns = query_ref.shape
@@ -185,28 +189,34 @@
         result = (state[2] / state[1]).astype(out_ref.dtype)
         for i in range(per_group):
             out_ref[:, pl.ds((g * per_group + i) * HD, HD)] = result[i * rows : (i + 1) * rows]
+        done(g)
 
 
 def front_kernel(
-    high, kv_in, meta_in, query_ref, weight_in, stream_ref, gain_ref,
+    high, key_in, value_in, ids_ref, gates_ref, query_ref, weight_in, stream_ref, gain_ref,
     mixed_ref, normed_ref, meta_all,
     kv_all, weights, context, contexts, part, mine, ready, landed,
     kv_r, meta_r, kv_s, meta_s, local, weight_sem, line_s, line_r, over_s, over_r, away_s, away_r
 ):
     h, l, e = split_position()
     mesh_id = pl.DeviceIdType.MESH
+    half = key_in.shape[1]
+    top = ids_ref.shape[1]
     copies = [
-        pltpu.make_async_copy(kv_in, kv_all.at[h, l], local.at[0]),
-        pltpu.make_async_copy(meta_in, meta_all.at[h, l, e], local.at[1]),
+        pltpu.make_async_copy(key_in, kv_all.at[h, l, :, pl.ds(0, half)], local.at[0]),
+        pltpu.make_async_copy(value_in, kv_all.at[h, l, :, pl.ds(half, half)], local.at[1]),
         pltpu.make_async_copy(weight_in, weights.at[l], local.at[2]),
     ]
     for one in copies:
         one.start()
+    meta_all[h, l, e] = jnp.zeros_like(meta_all[h, l, e])
+    meta_all[h, l, e, :, pl.ds(0, top)] = ids_ref[...].astype(jnp.float32)
+    meta_all[h, l, e, :, pl.ds(top, top)] = gates_ref[...]
     all_barrier(high, h, l, e)
     for one in copies:
         one.wait()
     gather_steps(
-        high, (kv_all, meta_all), (False, True), (1, 1), (kv_r, meta_r), (kv_s, meta_s), h, l, e
+        high, (kv_all, meta_all), (False, True), (2, 1), (kv_r, meta_r), (kv_s, meta_s), h, l, e
     )
     weight_copy = pltpu.make_async_remote_copy(
         src_ref=weights.at[l],
@@ -217,15 +227,11 @@
         device_id_type=mesh_id,
     )
     weight_copy.start()
-    attend(query_ref, kv_all, context, h * LOW + l)
-    own = pltpu.make_async_copy(context, contexts.at[h], local.at[0])
-    own.start()
-    own.wait()
-    parts = PARTS
-    rows = context.shape[0] // parts
+    parts = half // HD
+    columns = context.shape[1] // parts
 
     def hop(way, h0, c):
-        ref = contexts.at[h0, pl.ds(c * rows, rows)]
+        ref = contexts.at[h0, :, pl.ds(c * columns, columns)]
         return pltpu.make_async_remote_copy(
             src_ref=ref,
             dst_ref=ref,
@@ -245,8 +251,14 @@
             def _():
                 hop(1, h0, c).start()
 
-    for c in range(parts):
+    def done(c):
+        at = pl.ds(c * columns, columns)
+        own = pltpu.make_async_copy(context.at[:, at], contexts.at[h, :, at], local.at[0])
+        own.start()
+        own.wait()
         hops(h, c, True, True)
+
+    attend(query_ref, kv_all, context, h * LOW + l, done)
     for t in range(1, high):
         for c in range(parts):
             @pl.when(h - t >= 0)
@@ -313,15 +325,15 @@
         away((h + d) % high, (h + high - d) % high).wait_recv()
     squares = None
     for h0 in range(high):
-        columns = pl.ds(h0 * features, features)
-        value = stream_ref[:, columns].astype(jnp.float32) + landed[h0].astype(jnp.float32)
-        mixed_ref[:, columns] = value
+        block = pl.ds(h0 * features, features)
+        value = stream_ref[:, block].astype(jnp.float32) + landed[h0].astype(jnp.float32)
+        mixed_ref[:, block] = value
         term = jnp.sum(value * value, axis=-1, keepdims=True)
         squares = term if squares is None else squares + term
     factor = lax.rsqrt(squares / (high * features) + 1e-06)
     for h0 in range(high):
-        columns = pl.ds(h0 * features, features)
-        normed_ref[:, columns] = (mixed_ref[:, columns] * factor * gain_ref[:, columns]).astype(
+        block = pl.ds(h0 * features, features)
+        normed_ref[:, block] = (mixed_ref[:, block] * factor * gain_ref[:, block]).astype(
             normed_ref.dtype
         )
     weight_copy.wait_send()
@@ -339,7 +351,7 @@
         away((h + d) % high, h).wait_send()
 
 
-def front(kv, meta, queries, weight, stream, gain, high):
+def front(keys, values, ids, gates, queries, weight, stream, gain, high):
     whole = pl.BlockSpec(memory_space=pltpu.VMEM)
     span = queries.shape[0]
     rows = stream.shape[0]
@@ -351,12 +363,12 @@
         out_shape=(
             jax.ShapeDtypeStruct(stream.shape, jnp.float32),
             jax.ShapeDtypeStruct(stream.shape, kind),
-            jax.ShapeDtypeStruct((high, LOW, 2) + meta.shape, meta.dtype),
+            jax.ShapeDtypeStruct((high, LOW, 2, rows, 128), jnp.float32),
         ),
-        in_specs=[whole] * 6,
+        in_specs=[whole] * 8,
         out_specs=(whole,) * 3,
         scratch_shapes=[
-            pltpu.VMEM((high, LOW) + kv.shape, kind),
+            pltpu.VMEM((high, LOW, span, 2 * keys.shape[1]), kind),
             pltpu.VMEM((LOW,) + weight.shape, kind),
             pltpu.VMEM(queries.shape, kind),
             pltpu.VMEM((high,) + queries.shape, kind),
@@ -364,14 +376,14 @@
             pltpu.VMEM((high, rows, features), kind),
             pltpu.VMEM((high, rows, features), kind),
             pltpu.VMEM((high, rows, features), kind),
+            sem((high, LOW, 2, 2)),
             sem((high, LOW, 2, 1)),
-            sem((high, LOW, 2, 1)),
-            sem((4, high, LOW, 1)),
+            sem((4, high, LOW, 2)),
             sem((4, high, LOW, 1)),
             sem((3,)),
             sem((2,)),
-            sem((2, high, PARTS)),
-            sem((high, PARTS)),
+            sem((2, high, keys.shape[1] // HD)),
+            sem((high, keys.shape[1] // HD)),
             sem((high,)),
             sem((high,)),
             sem((high,)),
@@ -381,12 +393,12 @@
             collective_id=1, has_side_effects=True, vmem_limit_bytes=VMEM_LIMIT
         ),
         name="front",
-    )(kv, meta, queries, weight, stream, gain)
+    )(keys, values, ids, gates, queries, weight, stream, gain)
 
 
 def back_kernel(
-    high, parts, normed_ref, mixed_ref, choose_ref, combine_ref, first_hbm, second_hbm, out_ref,
-    every, first, second, picked, act, near, sums, across, running, line,
+    high, parts, top, normed_ref, mixed_ref, meta_ref, first_hbm, second_hbm, out_ref,
+    choose_ref, combine_ref, every, first, second, picked, act, near, sums, across, running, line,
     local, weight_sem, recv, send, near_s, near_r, across_s, across_r, line_s, line_r
 ):
     h, l, e = split_position()
@@ -403,7 +415,41 @@
     own.start()
     line_barrier(high, h, l, e)
     own.wait()
-    gather_steps(high, (every,), (True,), (parts,), (recv,), (send,), h, l, e)
+    device = (h * LOW + l) * 2 + e
+    tokens_here, total = combine_ref.shape[1:]
+    span = every.shape[3]
+
+    def build(h0):
+        meta = meta_ref[h0].reshape(tokens_here, 128)
+        moved = pltpu.roll(meta, 128 - top, axis=1)
+        lane = lax.broadcasted_iota(jnp.int32, meta.shape, 1)
+        chosen, gates, table = [], [], jnp.zeros_like(meta)
+        for i in range(experts):
+            here = (device * experts + i).astype(jnp.float32)
+            hit = (meta == here) & (lane < top)
+            chosen.append(jnp.sum(jnp.where(hit, 1.0, 0.0), axis=1, keepdims=True))
+            gates.append(jnp.sum(jnp.where(hit, moved, 0.0), axis=1, keepdims=True))
+            table = table + jnp.where(lane == i, chosen[i], 0.0)
+        square = (tokens_here, tokens_here)
+        row = lax.broadcasted_iota(jnp.int32, square, 0)
+        column = lax.broadcasted_iota(jnp.int32, square, 1)
+        earlier = jnp.where((column < row) & (row // span == column // span), 1.0, 0.0)
+        place = jnp.dot(
+            earlier.astype(jnp.bfloat16), table.astype(jnp.bfloat16), preferred_element_type=jnp.float32
+        )
+        wide = (tokens_here, -(-total // 128) * 128)
+        number = lax.broadcasted_iota(jnp.int32, wide, 1).astype(jnp.float32)
+        block = (lax.broadcasted_iota(jnp.int32, (tokens_here, 1), 0) // span).astype(jnp.float32)
+        onehot, weigh = jnp.zeros(wide, jnp.float32), jnp.zeros(wide, jnp.float32)
+        for i in range(experts):
+            within = jnp.sum(jnp.where(lane == i, place, 0.0), axis=1, keepdims=True)
+            match = (number == within + block * CAP + i * slots) & (chosen[i] > 0.5)
+            onehot = onehot + jnp.where(match, 1.0, 0.0)
+            weigh = weigh + jnp.where(match, gates[i], 0.0)
+        combine_ref[h0] = weigh[:, :total].astype(combine_ref.dtype)
+        choose_ref[h0] = jnp.transpose(onehot)[:total].astype(choose_ref.dtype)
+
+    gather_steps(high, (every,), (True,), (parts,), (recv,), (send,), h, l, e, build)
     for one in loads:
         one.wait()
     rows_all = every.shape[1] * every.shape[2] * every.shape[3]
@@ -579,7 +625,7 @@
             to_line(1, h0, c).wait_send()
 
 
-def back(normed, mixed, choose, combine, expert_in, expert_out, high):
+def back(normed, mixed, meta, expert_in, expert_out, high, top):
     rows, width = mixed.shape
     parts = PARTS
     whole = pl.BlockSpec(memory_space=pltpu.VMEM)
@@ -587,13 +633,16 @@
     kind = jnp.bfloat16
     sem = pltpu.SemaphoreType.DMA
     experts = expert_in.shape[0]
-    slots = choose.shape[1] // experts
+    slots = LOW * 2 * CAP
+    tokens = LOW * 2 * rows
     return pl.pallas_call(
-        functools.partial(back_kernel, high, parts),
+        functools.partial(back_kernel, high, parts, top),
         out_shape=jax.ShapeDtypeStruct((rows, width), kind),
-        in_specs=[whole] * 4 + [away] * 2,
+        in_specs=[whole] * 3 + [away] * 2,
         out_specs=whole,
         scratch_shapes=[
+            pltpu.VMEM((high, experts * slots, tokens), kind),
+            pltpu.VMEM((high, tokens, experts * slots), kind),
             pltpu.VMEM((high, LOW, 2, rows, width), kind),
             pltpu.VMEM(expert_in.shape, kind),
             pltpu.VMEM(expert_out.shape, kind),
@@ -616,7 +665,7 @@
             collective_id=2, has_side_effects=True, vmem_limit_bytes=VMEM_LIMIT
         ),
         name="back",
-    )(normed, mixed, choose, combine, expert_in, expert_out)
+    )(normed, mixed, meta, expert_in, expert_out)
 
 
 def on_device(
@@ -631,45 +680,12 @@
     expert_in,
     expert_out,
 ):
-    seq_count = lax.axis_size("seq")
-    exp_count = lax.axis_size("exp")
-    high = seq_count // LOW
-    local_rows = stream.shape[0]
-    top = expert_ids.shape[1]
-    meta = jnp.concatenate([expert_ids.astype(jnp.float32), gate_weights], axis=1)
-    meta = jnp.pad(meta, ((0, 0), (0, 128 - 2 * top)))
-    kv = jnp.concatenate([key_rows, value_rows], axis=1)
-    mixed, normed, all_meta = front(
-        kv, meta, queries, out_weight, stream, norm_gain.reshape(1, -1), high
+    high = lax.axis_size("seq") // LOW
+    mixed, normed, meta = front(
+        key_rows, value_rows, expert_ids, gate_weights, queries, out_weight, stream,
+        norm_gain.reshape(1, -1), high,
     )
-    local_experts = expert_in.shape[0]
-    device = lax.axis_index("seq") * exp_count + lax.axis_index("exp")
-    inner = LOW * exp_count
-    all_meta = all_meta.reshape(high * inner, local_rows, -1)
-    ids = all_meta[..., :top].astype(jnp.int32)
-    gates = all_meta[..., top : 2 * top]
-    here = device * local_experts + jnp.arange(local_experts, dtype=jnp.int32)
-    hit = ids[:, None, :, :] == here[None, :, None, None]
-    chosen = jnp.any(hit, axis=-1)
-    gate = jnp.sum(jnp.where(hit, gates[:, None], 0.0), axis=-1)
-    place = jnp.cumsum(chosen.astype(jnp.int32), axis=-1) - 1
-    place = jnp.where(chosen, place, -1).reshape(high, inner, local_experts, local_rows)
-    gate = gate.reshape(high, inner, local_experts, local_rows)
-    slot = jnp.arange(CAP, dtype=jnp.int32)
-    same = jnp.eye(inner, dtype=jnp.bool_)
-    choose = (
-        (place.transpose(0, 2, 1, 3)[:, :, None, None, :, :] == slot[None, None, None, :, None, None])
-        & same[None, None, :, None, :, None]
-    ).astype(jnp.bfloat16)
-    choose = choose.reshape(high, local_experts * inner * CAP, inner * local_rows)
-    weigh = jnp.where(
-        (place.transpose(0, 1, 3, 2)[:, :, :, :, None, None] == slot)
-        & same[None, :, None, None, :, None],
-        gate.transpose(0, 1, 3, 2)[:, :, :, :, None, None],
-        0.0,
-    ).astype(jnp.bfloat16)
-    combine = weigh.reshape(high, inner * local_rows, local_experts * inner * CAP)
-    return back(normed, mixed, choose, combine, expert_in, expert_out, high)
+    return back(normed, mixed, meta, expert_in, expert_out, high, expert_ids.shape[1])
 
 
 def solution(mesh):

time: 169 us -> 152 us (0.90)
  other arithmetic: 9.16 us -> 0 us
  Pallas kernels: 151 us -> 147 us
  local copies, waits for them, and re-layouts: 8.04 us -> 4.43 us
    pallas_call x1, Pallas kernels: 77.2 us -> 73.4 us  [front(): pl.pallas_call(functools.partial(front_kernel, high), out_shape=(jax.Shap...]
    another operation x1 -> x0, other arithmetic: 3.79 us -> none  [on_device(): place = jnp.cumsum(chosen.astype(jnp.int32), axis=-1) - 1]
    and x10 -> x0, local copies, waits for them, and re-layouts: 2.89 us -> none  [the longest x6 1.75 us: on_device(): (place.transpose(0, 1, 3, 2)[:, :, :, :, None, None] == slot) & same[None...]
    unnamed x2 -> x3, local copies, waits for them, and re-layouts: 1.85 us -> 4.43 us
    convert_element_type x5 -> x0, other arithmetic: 2.56 us -> none  [the longest x1 1.01 us: on_device(): weigh = jnp.where((place.transpose(0, 1, 3, 2)[:, :, :, :, None, None] ==...]
    concatenate x2 -> x0, other arithmetic: 2.22 us -> none  [the longest x1 1.53 us: on_device(): kv = jnp.concatenate([key_rows, value_rows], axis=1)]
where the time goes in v3:
time: 152 us
  Pallas kernels  147 us (97%)
  local copies, waits for them, and re-layouts  4.43 us (3%)
    pallas_call x1, Pallas kernels, back(): pl.pallas_call(functools.partial(back_kernel, high, parts, top), out_shap...  74.1 us
    pallas_call x1, Pallas kernels, front(): pl.pallas_call(functools.partial(front_kernel, high), out_shape=(jax.Shap...  73.4 us
    unnamed x3, local copies, waits for them, and re-layouts  4.43 us

profile of v3, /device:TPU:16, one launch (start us, length us, event | category | flops | bytes accessed | tf_op | source)
XLA Modules:
  0.0 151.9 jit_solution(4667959628495461863)
XLA Ops:
  0.0 1.4 copy.11.ids_ref
  1.4 1.4 copy.12.gates_ref
  2.8 73.4 %front.1 = (f32[64,2048]{1,0:T(8,128)}, bf16[64,2048]{1,0:T(8,128)(2,1)}, f32[4,2,2,64,128]{4,3,2,1,0:T(8,128)}) custom-call(bf16[128,256]{1,0:T(8,128)(2,1)} %key_in.1, bf16[128,256]{1,0:T(8,128)(2,1)} %value_in.1, s32[64,8]{1,0:T(8,128)} %copy.11.ids_ref, f32[64,8]{1,0:T(8,128)} %copy.12.gates_ref, bf16[128,2048]{1,0:T(8,128)(2,1)} %query_ref.1, ...), custom_call_target="tpu_custom_call" | custom-call | tf_op jit(solution)/shard_map/front/pallas_call | solution.py:361
  76.1 74.1 %back.1 = bf16[64,2048]{1,0:T(8,128)(2,1)} custom-call(bf16[64,2048]{1,0:T(8,128)(2,1)} %get-tuple-element.8.normed_ref, f32[64,2048]{1,0:T(8,128)} %get-tuple-element.9.mixed_ref, f32[4,2,2,64,128]{4,3,2,1,0:T(8,128)} %get-tuple-element.10.meta_ref, bf16[4,2048,1536]{2,1,0:T(8,128)(2,1)} %first_hbm.1, bf16[4,768,2048]{2,1,0:T(8,128)(2,1)} %second_hbm.1), custom_call_target="tpu_custom_call" | custom-call | tf_op jit(solution)/shard_map/back/pallas_call | solution.py:638
  150.2 1.7 %copy.14 = bf16[64,2048]{1,0:T(8,128)(2,1)} copy(bf16[64,2048]{1,0:T(8,128)(2,1)} %back.1) | data formatting | bytes 524288
